TPU v7x, 512 devices: a whole 4x4x16 slice. The times are simulated.
512 devices in a mesh: segment: 4 (over y), shard: 16 (over z), stream: 8 (over x, core).
Axes of the slice: x: 4, y: 4, z: 16, core: 2. Of those that a mesh axis runs over, the one named last changes fastest.
Arguments:
- latents: bfloat16 [32, 16, 16, 32, 256], P('stream', 'shard'), parts along dimension 0, may hold values from -6 to 6
- norm_gain: float32 [4, 256], P('segment'), may hold values from 0.25 to 1.75
- time_weight: bfloat16 [4, 3, 256, 256], P('segment'), may hold values from -0.21875 to 0.21875
- space_weight: bfloat16 [4, 9, 256, 256], P('segment'), may hold values from -0.125 to 0.125
- carry_in: bfloat16 [4, 16, 16, 32, 256], P('segment', 'stream', 'shard'), parts along dimension 1, may hold values from -6 to 6
Outputs:
- decoded: bfloat16 [32, 16, 16, 32, 256], P(('stream', 'segment'), 'shard'), parts along dimension 0
- carry_out: bfloat16 [4, 16, 16, 32, 256], P('segment', 'stream', 'shard'), parts along dimension 1
There are 8 independent parts, one for each index of `stream`. A program takes and returns all parts, laid end to end along the dimension named above; an argument that names none is the same for every part. Nothing has to cross between parts.
All inputs are finite; a program needn't handle non-finite values.
Results may differ from a plain program's by a relative error of at most 0.009.
Values may be sent and summed in bfloat16 or wider, within the bound.
No kernel may reach another device: no remote copies, remote signals or barrier semaphores. Data moves between devices by JAX's collectives and lax.ppermute only.
A program may use at most 64 MiB of HBM per device.

v0:
```python
import functools

import jax
import jax.numpy as jnp
from jax import lax
from jax.experimental import pallas as pl
from jax.experimental.pallas import tpu as pltpu
from jax.sharding import PartitionSpec as P


C = 256
LANES = 128
HALF = 128
TAPS = 12
GAIN_ROW = TAPS * HALF
PACKED = GAIN_ROW + 16
SECTIONS = 4
F32 = jnp.float32
BF16 = jnp.bfloat16

VMEM = pl.BlockSpec(memory_space=pltpu.VMEM)
HBM = pl.BlockSpec(memory_space=pltpu.HBM)
SMEM = pl.BlockSpec(memory_space=pltpu.SMEM)


def shape_of(*dims, dtype=BF16):
    return jax.ShapeDtypeStruct(dims, dtype)


def call(kernel, outs, in_specs, scratch=(), flops=1 << 20, moved=1 << 20, room=16):
    out_specs = tuple(VMEM for _ in outs) if isinstance(outs, tuple) else VMEM
    return pl.pallas_call(
        kernel,
        out_shape=outs,
        in_specs=in_specs,
        out_specs=out_specs,
        scratch_shapes=list(scratch),
        cost_estimate=pl.CostEstimate(flops=flops, bytes_accessed=moved, transcendentals=0),
        compiler_params=pltpu.CompilerParams(vmem_limit_bytes=room << 20),
    )


def chunk_kernel(columns, row, out):
    flat = columns[...].reshape(16, 32, C)
    for side in range(2):
        lanes = slice(side * LANES, (side + 1) * LANES)
        out[:, side * 32 : side * 32 + 32, :] = flat[:, :, lanes]
        for frame in range(2):
            at = 64 + 4 * side + 2 * frame
            for z in range(16):
                out[z, at : at + 2, :] = row[frame, 2 * z : 2 * z + 2, lanes]


def pack_kernel(scal, gain, taps_time, taps_space, out, sems):
    at = pl.multiple_of(scal[1] * HALF, HALF)
    copies = []
    for tap in range(TAPS):
        own = taps_time.at[0, tap] if tap < 3 else taps_space.at[0, tap - 3]
        copies.append(
            pltpu.make_async_copy(own.at[pl.ds(at, HALF)], out.at[pl.ds(tap * HALF, HALF)], sems.at[tap])
        )
        copies[-1].start()
    value = gain[...]
    high = value.astype(BF16)
    rest = value - high.astype(F32)
    middle = rest.astype(BF16)
    low = (rest - middle.astype(F32)).astype(BF16)
    pick = lax.broadcasted_iota(jnp.int32, (16, C), 0)
    rows = jnp.where(pick == 0, high.astype(F32), 0.0)
    rows = jnp.where(pick == 1, middle.astype(F32), rows)
    rows = jnp.where(pick == 2, low.astype(F32), rows)
    for copy in copies:
        copy.wait()
    out[GAIN_ROW:PACKED, :] = rows.astype(BF16)


def unpack_kernel(got, frames, before, carry):
    for side in range(2):
        lanes = slice(side * LANES, (side + 1) * LANES)
        block = got[:, side * 32 : side * 32 + 32, :]
        frames[:, :, lanes] = block
        before[:, :, lanes] = block[8:16]
        for n in range(4):
            frame, col = n // 2, n % 2
            carry[frame, col * 16 : col * 16 + 16, lanes] = got[:, 64 + 4 * side + n, :]


def fetch(section, scal, own, bufs, out, terms, sems, gain_sem):
    mine, core = scal[0], scal[1]
    rel = lax.rem(section - mine + SECTIONS, SECTIONS)
    plan = []
    for tap in range(TAPS):
        for side in range(2):
            at = pl.multiple_of((core if side == 0 else 1 - core) * HALF, HALF)
            plan.append((tap, side, at, out.at[tap, pl.ds(at, HALF)]))
    taps_time, taps_space = own

    @pl.when(rel == 0)
    def _():
        for tap, side, at, dst in plan:
            src = taps_time.at[0, tap] if tap < 3 else taps_space.at[0, tap - 3]
            pltpu.make_async_copy(src.at[pl.ds(at, HALF)], dst, sems.at[tap, side]).start()
        pltpu.make_async_copy(bufs[0].at[pl.ds(GAIN_ROW, 16)], terms, gain_sem).start()

    for which in range(3):

        @pl.when(rel == which + 1)
        def _(which=which):
            for tap, side, at, dst in plan:
                src = bufs[2 * which + side].at[pl.ds(tap * HALF, HALF)]
                pltpu.make_async_copy(src, dst, sems.at[tap, side]).start()
            pltpu.make_async_copy(bufs[2 * which].at[pl.ds(GAIN_ROW, 16)], terms, gain_sem).start()

    def wait(first, last):
        for tap, side, at, dst in plan:
            if first <= tap < last:
                pltpu.make_async_copy(
                    bufs[side].at[pl.ds(tap * HALF, HALF)], dst, sems.at[tap, side]
                ).wait()

    def gain_row(gain):
        pltpu.make_async_copy(bufs[0].at[pl.ds(GAIN_ROW, 16)], terms, gain_sem).wait()
        rows = terms[...].astype(F32)
        received = rows[0:1] + (rows[1:2] + rows[2:3])
        return jnp.where(rel == 0, gain[...], received)

    return wait, gain_row


def normed_of(values, gain_row):
    inverse = lax.rsqrt(jnp.mean(values * values, axis=-1, keepdims=True) + 1e-06)
    return (values * inverse * gain_row).astype(BF16)


def pieces(count, size):
    return [(at, min(size, count - at)) for at in range(0, count, size)]


def mix(source, weights, hidden, count, columns):
    taps = weights[0:3].reshape(3 * C, C)
    rows = columns * 16
    for at, size in pieces(count, 4):
        parts = [source[at + k : at + k + size, 0:rows].reshape(size * rows, C) for k in range(3)]
        mixed = jnp.dot(jnp.concatenate(parts, axis=-1), taps, preferred_element_type=F32)
        value = jax.nn.silu(mixed).astype(BF16).reshape(size, rows, C)
        for col in range(columns):
            hidden[col, at : at + size] = value[:, col * 16 : col * 16 + 16, :]


def spatial(hidden, weights, col, count):
    size = count * 16
    row = lax.broadcasted_iota(jnp.int32, (size, C), 0) % 16
    lhs = jnp.concatenate([hidden[col + q, 0:count].reshape(size, C) for q in range(3)], axis=-1)
    y = []
    for p in range(3):
        taps = weights[3 + 3 * p : 6 + 3 * p].reshape(3 * C, C)
        y.append(jnp.dot(lhs, taps, preferred_element_type=F32))
    down = jnp.where(row == 0, 0.0, pltpu.roll(y[0], 1, 0))
    up = jnp.where(row == 15, 0.0, pltpu.roll(y[2], size - 1, 0))
    return y[1] + down + up


def cols(col):
    return slice(col * 16, col * 16 + 16)


def pair_kernel(first, scal, gain, far, mid, left, right, *rest):
    if first:
        refs, (out, tails) = rest[:8], rest[8:10]
    else:
        refs, (out,) = rest[:8], rest[8:9]
    own, bufs = refs[:2], refs[2:]
    weights, terms, sems, gain_sem, normed, hidden, second, normed2 = rest[(10 if first else 9) :]
    section = 0 if first else 2
    total = 24 if first else 20
    mine, shard, shards = scal[0], scal[2], scal[3]
    loads = []
    for k in range(2):
        loads.append(
            fetch(section + k, scal, own, bufs, weights.at[k], terms.at[k], sems.at[k], gain_sem.at[k])
        )
    if first:
        mine_rel = lax.rem(2 - mine + SECTIONS, SECTIONS)
        for which in range(3):

            @pl.when(lax.rem(mine_rel + 2, 3) == which)
            def _(which=which):
                pltpu.make_async_copy(
                    bufs[2 * which].at[pl.ds(GAIN_ROW, 16)], terms.at[2], gain_sem.at[2]
                ).start()

    row = loads[0][1](gain)
    sources = (left, mid, right)
    for n, source in enumerate(sources):
        for at, size in pieces(total, 8):
            values = source[at : at + size].astype(F32).reshape(size * 32, C)
            normed[at : at + size, n * 32 : n * 32 + 32] = normed_of(values, row).reshape(size, 32, C)
    if first:
        tails[0] = normed[total - 2 : total, 32:64]

    @pl.when(mine == 0)
    def _():
        for n, source in enumerate(sources):
            normed[total - 18 : total - 16, n * 32 : n * 32 + 32] = source[total - 18 : total - 16]

    loads[0][0](0, 3)
    count = total - 2
    mix(normed, weights.at[0], hidden, count, 6)
    loads[0][0](3, TAPS)
    row = loads[1][1](gain)
    for col in range(4):
        source, at = ((left, cols(1)), (mid, cols(0)), (mid, cols(1)), (right, cols(0)))[col]
        a = source[2:, at, :].reshape(count * 16, C).astype(F32)
        result = (a + spatial(hidden, weights.at[0], col, count)).astype(BF16)
        if col in (1, 2):
            second[:, cols(col - 1), :] = result.reshape(count, 16, C)
        n = normed_of(result.astype(F32), row)
        if col == 0:
            n = jnp.where(shard == 0, jnp.zeros_like(n), n)
        if col == 3:
            n = jnp.where(shard == shards - 1, jnp.zeros_like(n), n)
        normed2[:, cols(col), :] = n.reshape(count, 16, C)
    own_tail = normed2[count - 2 : count, 16:48]
    if first:
        tails[1] = own_tail

    @pl.when(mine == 0)
    def _():
        for col in range(4):
            source, at = ((left, cols(1)), (mid, cols(0)), (mid, cols(1)), (right, cols(0)))[col]
            normed2[count - 18 : count - 16, cols(col)] = source[total - 20 : total - 18, at, :]

    loads[1][0](0, 3)
    count = total - 4
    mix(normed2, weights.at[1], hidden, count, 4)
    loads[1][0](3, TAPS)
    for col in range(2):
        a = second[2:, cols(col), :].reshape(count * 16, C).astype(F32)
        result = (a + spatial(hidden, weights.at[1], col, count)).astype(BF16).reshape(count, 16, C)
        if first:
            out[:, cols(col), :] = result
        else:
            for side in range(2):
                lanes = slice(side * LANES, (side + 1) * LANES)
                out[:, side * 32 + col * 16 : side * 32 + col * 16 + 16, :] = result[:, :, lanes]
    if first:
        pltpu.make_async_copy(bufs[0].at[pl.ds(GAIN_ROW, 16)], terms.at[2], gain_sem.at[2]).wait()
        rows = terms[2].astype(F32)
        received = rows[0:1] + (rows[1:2] + rows[2:3])
        row = jnp.where(mine == 2, gain[...], received)
        last = out[count - 2 : count].astype(F32).reshape(64, C)
        tails[2] = normed_of(last, row).reshape(2, 32, C)

        @pl.when(mine == 0)
        def _():
            out[0:4] = far[...]

    else:
        carry = jnp.where(mine == SECTIONS - 1, own_tail, far[...])
        for side in range(2):
            lanes = slice(side * LANES, (side + 1) * LANES)
            for n in range(4):
                out[:, 64 + 4 * side + n, :] = carry[n // 2, cols(n % 2), lanes]


def pair_call(first, scal, gain, far, sources, own, bufs):
    total = 24 if first else 20
    count = total - 2
    if first:
        outs = (shape_of(20, 32, C), shape_of(3, 2, 32, C))
    else:
        outs = shape_of(16, 72, LANES)
    return call(
        functools.partial(pair_kernel, first),
        outs,
        [SMEM] + [VMEM] * 5 + [HBM] * 8,
        [
            pltpu.VMEM((2, TAPS, C, C), BF16),
            pltpu.VMEM((3, 16, C), BF16),
            pltpu.SemaphoreType.DMA((2, TAPS, 2)),
            pltpu.SemaphoreType.DMA((3,)),
            pltpu.VMEM((total, 96, C), BF16),
            pltpu.VMEM((6, count, 16, C), BF16),
            pltpu.VMEM((count, 32, C), BF16),
            pltpu.VMEM((count, 64, C), BF16),
        ],
        flops=1 << 31,
        moved=4 << 20,
        room=58,
    )(scal, gain, far, *sources, *own, *bufs)


def join_kernel(scal, frames, before, near, carry, out):
    out[8:24] = frames[...]
    out[0:8] = before[...]

    @pl.when(scal[0] == 0)
    def _():
        out[4:6] = near[...]
        out[6:8] = carry[...]


def body(latents, norm_gain, time_weight, space_weight, carry_in):
    shards = lax.axis_size("shard")
    streams = lax.axis_size("stream")
    mine = lax.axis_index("segment")
    core = lax.rem(lax.axis_index("stream"), 2)
    here = lax.axis_index("shard")
    scal = jnp.stack([mine, core, here, jnp.int32(shards)]).astype(jnp.int32)

    def ring(distance):
        return [(i, (i + distance) % SECTIONS) for i in range(SECTIONS)]

    def over_segments(array, pairs):
        return lax.ppermute(array, "segment", pairs)

    swap = [(i, i ^ 1) for i in range(streams)]
    up = [(i, i + 1) for i in range(shards - 1)]
    down = [(i + 1, i) for i in range(shards - 1)]

    block = lax.dynamic_index_in_dim(latents, mine, 0, keepdims=False)[0]
    chunks = call(chunk_kernel, shape_of(16, 72, LANES), [VMEM] * 2)(
        block.transpose(1, 0, 2), carry_in[0, :, 0]
    )
    got = lax.all_to_all(chunks, "shard", split_axis=0, concat_axis=0, tiled=True)

    packed = call(
        pack_kernel,
        shape_of(PACKED, C),
        [SMEM, VMEM, HBM, HBM],
        [pltpu.SemaphoreType.DMA((TAPS,))],
        room=58,
    )(scal, norm_gain, time_weight, space_weight)
    bufs = []
    for distance in (-1, 2, 1):
        buf = over_segments(packed, ring(distance))
        bufs += [buf, lax.ppermute(buf, "stream", swap)]

    frames, sent_before, carry = call(
        unpack_kernel, (shape_of(16, 32, C), shape_of(8, 32, C), shape_of(2, 32, C)), [VMEM]
    )(got)
    before = over_segments(sent_before, [(0, 1), (1, 2), (2, 3)])
    near = over_segments(carry, [(1, 0), (3, 2)])
    far = over_segments(jnp.concatenate([near, carry], axis=0), [(2, 0)])
    joined = call(join_kernel, shape_of(24, 32, C), [SMEM] + [VMEM] * 4)(
        scal, frames, before, near, carry
    )

    def beside(array):
        came_left = lax.ppermute(array, "shard", up)
        came_right = lax.ppermute(array, "shard", down)
        return array, came_left, came_right

    own = (time_weight, space_weight)
    middle, tails = pair_call(True, scal, norm_gain, far, beside(joined), own, bufs)
    sources = beside(middle)
    over = over_segments(tails[1:3].reshape(4, 32, C), [(3, 2)])
    wrapped = over_segments(jnp.where(mine == 3, tails[0], over[0:2]), [(3, 0), (2, 1)])
    carry = jnp.where(mine == 2, over[2:4], wrapped)
    out = pair_call(False, scal, norm_gain, carry, sources, own, bufs)
    sent = lax.all_to_all(out, "shard", split_axis=0, concat_axis=0, tiled=True)
    main = jnp.concatenate([sent[:, 0:32], sent[:, 32:64]], axis=-1)
    decoded = main.reshape(32, 16, C).transpose(1, 0, 2)[None, None]
    kept_rows = jnp.concatenate([sent[:, 64:68], sent[:, 68:72]], axis=-1)
    carry_out = kept_rows.reshape(shards, 2, 2, C).transpose(1, 0, 2, 3).reshape(1, 2, 1, 32, C)
    return (decoded, carry_out)


def solution(mesh):
    placed = (
        P("stream", "shard", None, None, None),
        P("segment", None),
        P("segment", None, None, None),
        P("segment", None, None, None),
        P("segment", "stream", "shard", None, None),
    )
    return jax.shard_map(
        body,
        mesh=mesh,
        in_specs=placed,
        out_specs=(
            P(("stream", "segment"), "shard", None, None, None),
            P("segment", "stream", "shard", None, None),
        ),
        check_vma=False,
    )
```

profile of v0, /device:TPU:32, one launch (start us, length us, event | category | flops | bytes accessed | tf_op | source)
XLA Modules:
  0.0 161.0 jit_solution(7883899951510899667)
XLA Ops:
  0.6 0.0 copy-start
  0.6 1.2 copy-done
  1.9 0.2 copy.13
  2.0 0.0 copy-start.2
  2.1 0.7 copy-done.2
  2.8 0.8 shard_map.68
  3.6 15.2 %all-to-all-start = ((bf16[16,72,128]{2,1,0:T(8,128)(2,1)}), bf16[16,72,128]{2,1,0:T(8,128)(2,1)S(1)}, u32[]{:S(2)}, u32[]{:S(2)}) async-start(bf16[16,72,128]{2,1,0:T(8,128)(2,1)} %shard_map.68), calls=%async_computation | async-start | bytes 589824 | tf_op jit(solution)/shard_map/all_to_all | solution.py:325
  18.8 0.7 pad_add_fusion.scal
  19.4 3.0 %shard_map.71 = bf16[1552,256]{1,0:T(8,128)(2,1)} custom-call(s32[4]{0:T(128)} %pad_add_fusion.scal, f32[1,256]{1,0:T(1,128)} %gain.5, bf16[1,3,256,256]{3,2,1,0:T(8,128)(2,1)} %rest_0_.3, bf16[1,9,256,256]{3,2,1,0:T(8,128)(2,1)} %rest_1_.3), custom_call_target="tpu_custom_call" | custom-call | flops 1048576 | bytes 1048576 | tf_op jit(solution)/shard_map/pallas_call | solution.py:327
  22.4 3.5 %collective-permute-start.9 = (bf16[1552,256]{1,0:T(8,128)(2,1)}, bf16[1552,256]{1,0:T(8,128)(2,1)S(1)}, u32[]{:S(2)}, u32[]{:S(2)}) collective-permute-start(bf16[1552,256]{1,0:T(8,128)(2,1)} %shard_map.71), channel_id=1, source_target_pairs={{0,128},{128,256},{256,384},{384,0},{1,129},{129,257},{257,385},{3... | collective-permute-start | bytes 2383880 | tf_op jit(solution)/shard_map/ppermute | solution.py:315
  25.9 3.6 %collective-permute-start.5 = (bf16[1552,256]{1,0:T(8,128)(2,1)}, bf16[1552,256]{1,0:T(8,128)(2,1)S(1)}, u32[]{:S(2)}, u32[]{:S(2)}) collective-permute-start(bf16[1552,256]{1,0:T(8,128)(2,1)} %shard_map.71), channel_id=1, source_target_pairs={{0,384},{128,0},{256,128},{384,256},{1,385},{129,1},{257,129},{385... | collective-permute-start | bytes 2383880 | tf_op jit(solution)/shard_map/ppermute | solution.py:315
  29.5 3.9 %collective-permute-start.7 = (bf16[1552,256]{1,0:T(8,128)(2,1)}, bf16[1552,256]{1,0:T(8,128)(2,1)}, u32[]{:S(2)}, u32[]{:S(2)}) collective-permute-start(bf16[1552,256]{1,0:T(8,128)(2,1)} %shard_map.71), channel_id=1, source_target_pairs={{0,256},{128,384},{256,0},{384,128},{1,257},{129,385},{257,1},{385... | collective-permute-start | bytes 2383880 | tf_op jit(solution)/shard_map/ppermute | solution.py:315
  33.4 11.8 %collective-permute-done.9.rest_6_ = bf16[1552,256]{1,0:T(8,128)(2,1)S(1)} collective-permute-done((bf16[1552,256]{1,0:T(8,128)(2,1)}, bf16[1552,256]{1,0:T(8,128)(2,1)S(1)}, u32[]{:S(2)}, u32[]{:S(2)}) %collective-permute-start.9) | collective-permute-done | bytes 794656 | tf_op jit(solution)/shard_map/ppermute | solution.py:315
  45.2 1.9 %collective-permute-start.10 = (bf16[1552,256]{1,0:T(8,128)(2,1)S(1)}, bf16[1552,256]{1,0:T(8,128)(2,1)}, u32[]{:S(2)}, u32[]{:S(2)}) collective-permute-start(bf16[1552,256]{1,0:T(8,128)(2,1)S(1)} %collective-permute-done.9.rest_6_), channel_id=1, source_target_pairs={{0,1},{1,0},{2,3},{3,2},{4,5},{5,4},{6,7},{7,6},{8,9},{9,8},{10,11... | collective-permute-start | bytes 2383880 | tf_op jit(solution)/shard_map/ppermute | solution.py:337
  47.1 1.5 collective-permute-done.5.rest_2_
  48.6 1.9 %collective-permute-start.6 = (bf16[1552,256]{1,0:T(8,128)(2,1)S(1)}, bf16[1552,256]{1,0:T(8,128)(2,1)}, u32[]{:S(2)}, u32[]{:S(2)}) collective-permute-start(bf16[1552,256]{1,0:T(8,128)(2,1)S(1)} %collective-permute-done.5.rest_2_), channel_id=1, source_target_pairs={{0,1},{1,0},{2,3},{3,2},{4,5},{5,4},{6,7},{7,6},{8,9},{9,8},{10,11... | collective-permute-start | bytes 2383880 | tf_op jit(solution)/shard_map/ppermute | solution.py:337
  50.5 12.5 %collective-permute-done.7.rest_4_ = bf16[1552,256]{1,0:T(8,128)(2,1)} collective-permute-done((bf16[1552,256]{1,0:T(8,128)(2,1)}, bf16[1552,256]{1,0:T(8,128)(2,1)}, u32[]{:S(2)}, u32[]{:S(2)}) %collective-permute-start.7) | collective-permute-done | bytes 794656 | tf_op jit(solution)/shard_map/ppermute | solution.py:315
  63.0 1.9 %collective-permute-start.8 = (bf16[1552,256]{1,0:T(8,128)(2,1)}, bf16[1552,256]{1,0:T(8,128)(2,1)}, u32[]{:S(2)}, u32[]{:S(2)}) collective-permute-start(bf16[1552,256]{1,0:T(8,128)(2,1)} %collective-permute-done.7.rest_4_), channel_id=1, source_target_pairs={{0,1},{1,0},{2,3},{3,2},{4,5},{5,4},{6,7},{7,6},{8,9},{9,8},{10,11... | collective-permute-start | bytes 2383880 | tf_op jit(solution)/shard_map/ppermute | solution.py:337
  64.9 0.1 shard_map.69
  65.0 1.3 collective-permute-start
  66.3 5.0 %collective-permute-start.2 = (bf16[8,32,256]{2,1,0:T(8,128)(2,1)S(1)}, bf16[8,32,256]{2,1,0:T(8,128)(2,1)S(1)}, u32[]{:S(2)}, u32[]{:S(2)}) collective-permute-start(bf16[8,32,256]{2,1,0:T(8,128)(2,1)S(1)} %get-tuple-element.9), channel_id=1, source_target_pairs={{0,128},{128,256},{256,384},{1,129},{129,257},{257,385},{2,130},{1... | collective-permute-start | bytes 393224 | tf_op jit(solution)/shard_map/ppermute | solution.py:315
  71.3 0.1 collective-permute-done.near
  71.4 1.3 collective-permute-start.1
  72.7 2.0 %collective-permute-done.2.before = bf16[8,32,256]{2,1,0:T(8,128)(2,1)S(1)} collective-permute-done((bf16[8,32,256]{2,1,0:T(8,128)(2,1)S(1)}, bf16[8,32,256]{2,1,0:T(8,128)(2,1)S(1)}, u32[]{:S(2)}, u32[]{:S(2)}) %collective-permute-start.2) | collective-permute-done | bytes 131104 | tf_op jit(solution)/shard_map/ppermute | solution.py:315
  74.7 0.6 shard_map.70.mid
  75.3 3.4 %collective-permute-start.3 = (bf16[24,32,256]{2,1,0:T(8,128)(2,1)S(1)}, bf16[24,32,256]{2,1,0:T(8,128)(2,1)S(1)}, u32[]{:S(2)}, u32[]{:S(2)}) collective-permute-start(bf16[24,32,256]{2,1,0:T(8,128)(2,1)S(1)} %shard_map.70.mid), channel_id=1, source_target_pairs={{0,8},{8,16},{16,24},{24,32},{32,40},{40,48},{48,56},{56,64},{64,7... | collective-permute-start | bytes 1179656 | tf_op jit(solution)/shard_map/ppermute | solution.py:350
  78.7 2.2 %collective-permute-done.1.far = bf16[4,32,256]{2,1,0:T(8,128)(2,1)S(1)} collective-permute-done((bf16[4,32,256]{2,1,0:T(8,128)(2,1)S(1)}, bf16[4,32,256]{2,1,0:T(8,128)(2,1)S(1)}, u32[]{:S(2)}, u32[]{:S(2)}) %collective-permute-start.1) | collective-permute-done | bytes 65568 | tf_op jit(solution)/shard_map/ppermute | solution.py:315
  80.9 2.3 %collective-permute-start.4 = (bf16[24,32,256]{2,1,0:T(8,128)(2,1)S(1)}, bf16[24,32,256]{2,1,0:T(8,128)(2,1)S(1)}, u32[]{:S(2)}, u32[]{:S(2)}) collective-permute-start(bf16[24,32,256]{2,1,0:T(8,128)(2,1)S(1)} %shard_map.70.mid), channel_id=1, source_target_pairs={{8,0},{16,8},{24,16},{32,24},{40,32},{48,40},{56,48},{64,56},{72,6... | collective-permute-start | bytes 1179656 | tf_op jit(solution)/shard_map/ppermute | solution.py:351
  83.2 0.0 collective-permute-done.10.rest_7_
  83.2 0.0 collective-permute-done.8.rest_5_
  83.2 4.6 %collective-permute-done.3.left = bf16[24,32,256]{2,1,0:T(8,128)(2,1)S(1)} collective-permute-done((bf16[24,32,256]{2,1,0:T(8,128)(2,1)S(1)}, bf16[24,32,256]{2,1,0:T(8,128)(2,1)S(1)}, u32[]{:S(2)}, u32[]{:S(2)}) %collective-permute-start.3) | collective-permute-done | bytes 393248 | tf_op jit(solution)/shard_map/ppermute | solution.py:350
  87.8 5.0 %collective-permute-done.4.right = bf16[24,32,256]{2,1,0:T(8,128)(2,1)S(1)} collective-permute-done((bf16[24,32,256]{2,1,0:T(8,128)(2,1)S(1)}, bf16[24,32,256]{2,1,0:T(8,128)(2,1)S(1)}, u32[]{:S(2)}, u32[]{:S(2)}) %collective-permute-start.4) | collective-permute-done | bytes 393248 | tf_op jit(solution)/shard_map/ppermute | solution.py:351
  92.9 0.7 copy-done.7
  93.6 9.4 %shard_map.72 = (bf16[20,32,256]{2,1,0:T(8,128)(2,1)}, bf16[3,2,32,256]{3,2,1,0:T(8,128)(2,1)}) custom-call(s32[4]{0:T(128)} %pad_add_fusion.scal, f32[1,256]{1,0:T(1,128)} %gain.5, bf16[4,32,256]{2,1,0:T(8,128)(2,1)} %copy-done.10, bf16[24,32,256]{2,1,0:T(8,128)(2,1)} %copy-done.1, bf16[24,32,256]{2,1,0:T(8,128)(2,1)} %copy-done.6, ...), custom_call_target="tpu_custom_call" | custom-call | flops 2147483648 | bytes 4194304 | tf_op jit(solution)/shard_map/pallas_call | solution.py:273
  103.0 0.8 slice.24
  103.9 0.7 collective-permute-start.11
  104.5 3.4 %collective-permute-start.13 = (bf16[20,32,256]{2,1,0:T(8,128)(2,1)}, bf16[20,32,256]{2,1,0:T(8,128)(2,1)S(1)}, u32[]{:S(2)}, u32[]{:S(2)}) collective-permute-start(bf16[20,32,256]{2,1,0:T(8,128)(2,1)} %get-tuple-element.11.mid), channel_id=1, source_target_pairs={{0,8},{8,16},{16,24},{24,32},{32,40},{40,48},{48,56},{56,64},{64,7... | collective-permute-start | bytes 983048 | tf_op jit(solution)/shard_map/ppermute | solution.py:350
  107.9 2.5 %collective-permute-start.14 = (bf16[20,32,256]{2,1,0:T(8,128)(2,1)}, bf16[20,32,256]{2,1,0:T(8,128)(2,1)S(1)}, u32[]{:S(2)}, u32[]{:S(2)}) collective-permute-start(bf16[20,32,256]{2,1,0:T(8,128)(2,1)} %get-tuple-element.11.mid), channel_id=1, source_target_pairs={{8,0},{16,8},{24,16},{32,24},{40,32},{48,40},{56,48},{64,56},{72,6... | collective-permute-start | bytes 983048 | tf_op jit(solution)/shard_map/ppermute | solution.py:351
  110.4 0.8 slice_select_fusion
  111.2 1.3 collective-permute-start.12
  112.5 6.6 %collective-permute-done.12 = bf16[2,32,256]{2,1,0:T(8,128)(2,1)S(1)} collective-permute-done((bf16[2,32,256]{2,1,0:T(8,128)(2,1)S(1)}, bf16[2,32,256]{2,1,0:T(8,128)(2,1)S(1)}, u32[]{:S(2)}, u32[]{:S(2)}) %collective-permute-start.12) | collective-permute-done | bytes 32800 | tf_op jit(solution)/shard_map/ppermute | solution.py:315
  119.1 0.6 slice_select_fusion.1.far
  119.7 0.7 copy-done.8
  120.5 0.7 copy-done.9
  121.2 8.3 %shard_map.73 = bf16[16,72,128]{2,1,0:T(8,128)(2,1)} custom-call(s32[4]{0:T(128)} %pad_add_fusion.scal, f32[1,256]{1,0:T(1,128)} %gain.5, bf16[2,32,256]{2,1,0:T(8,128)(2,1)} %slice_select_fusion.1.far, bf16[20,32,256]{2,1,0:T(8,128)(2,1)} %get-tuple-element.11.mid, bf16[20,32,256]{2,1,0:T(8,128)(2,1)} %copy-done.8, bf16[20,32,256]{2,1,0:T(8,128)(2,1)} %copy-done.9, ...), custom_call_target="tpu_custom_call" | custom-call | flops 2147483648 | bytes 4194304 | tf_op jit(solution)/shard_map/pallas_call | solution.py:273
  129.6 29.9 %all_to_all.10 = bf16[16,72,128]{2,1,0:T(8,128)(2,1)S(1)} all-to-all(bf16[16,72,128]{2,1,0:T(8,128)(2,1)} %shard_map.73), channel_id=1, replica_groups=mesh['segment'=4,'shard'=16,'stream'=8] {'shard'}, dimensions={0} | all-to-all | bytes 589824 | tf_op jit(solution)/shard_map/all_to_all | solution.py:361
  159.5 0.6 reshape.20
  160.2 0.8 copy.12
  (28 shorter events, 0.2 us)
Async XLA Ops:
  0.6 1.2 copy-start
  2.0 0.8 copy-start.2
  3.6 61.3 %all-to-all-start = ((bf16[16,72,128]{2,1,0:T(8,128)(2,1)}), bf16[16,72,128]{2,1,0:T(8,128)(2,1)S(1)}, u32[]{:S(2)}, u32[]{:S(2)}) async-start(bf16[16,72,128]{2,1,0:T(8,128)(2,1)} %shard_map.68), calls=%async_computation | async-start | bytes 589824 | tf_op jit(solution)/shard_map/all_to_all | solution.py:325
  19.4 55.2 %copy-start.3 = (s32[4]{0:T(128)S(1)}, s32[4]{0:T(128)}, u32[]{:S(2)}) copy-start(s32[4]{0:T(128)} %pad_add_fusion.scal) | copy-start | bytes 52
  22.4 22.8 %collective-permute-start.9 = (bf16[1552,256]{1,0:T(8,128)(2,1)}, bf16[1552,256]{1,0:T(8,128)(2,1)S(1)}, u32[]{:S(2)}, u32[]{:S(2)}) collective-permute-start(bf16[1552,256]{1,0:T(8,128)(2,1)} %shard_map.71), channel_id=1, source_target_pairs={{0,128},{128,256},{256,384},{384,0},{1,129},{129,257},{257,385},{3... | collective-permute-start | bytes 2383880 | tf_op jit(solution)/shard_map/ppermute | solution.py:315
  25.9 22.7 %collective-permute-start.5 = (bf16[1552,256]{1,0:T(8,128)(2,1)}, bf16[1552,256]{1,0:T(8,128)(2,1)S(1)}, u32[]{:S(2)}, u32[]{:S(2)}) collective-permute-start(bf16[1552,256]{1,0:T(8,128)(2,1)} %shard_map.71), channel_id=1, source_target_pairs={{0,384},{128,0},{256,128},{384,256},{1,385},{129,1},{257,129},{385... | collective-permute-start | bytes 2383880 | tf_op jit(solution)/shard_map/ppermute | solution.py:315
  29.5 33.5 %collective-permute-start.7 = (bf16[1552,256]{1,0:T(8,128)(2,1)}, bf16[1552,256]{1,0:T(8,128)(2,1)}, u32[]{:S(2)}, u32[]{:S(2)}) collective-permute-start(bf16[1552,256]{1,0:T(8,128)(2,1)} %shard_map.71), channel_id=1, source_target_pairs={{0,256},{128,384},{256,0},{384,128},{1,257},{129,385},{257,1},{385... | collective-permute-start | bytes 2383880 | tf_op jit(solution)/shard_map/ppermute | solution.py:315
  45.2 47.6 %copy-start.4 = (bf16[1552,256]{1,0:T(8,128)(2,1)}, bf16[1552,256]{1,0:T(8,128)(2,1)S(1)}, u32[]{:S(2)}) copy-start(bf16[1552,256]{1,0:T(8,128)(2,1)S(1)} %collective-permute-done.9.rest_6_) | copy-start | bytes 2383876
  45.2 38.0 %collective-permute-start.10 = (bf16[1552,256]{1,0:T(8,128)(2,1)S(1)}, bf16[1552,256]{1,0:T(8,128)(2,1)}, u32[]{:S(2)}, u32[]{:S(2)}) collective-permute-start(bf16[1552,256]{1,0:T(8,128)(2,1)S(1)} %collective-permute-done.9.rest_6_), channel_id=1, source_target_pairs={{0,1},{1,0},{2,3},{3,2},{4,5},{5,4},{6,7},{7,6},{8,9},{9,8},{10,11... | collective-permute-start | bytes 2383880 | tf_op jit(solution)/shard_map/ppermute | solution.py:337
  48.6 44.2 %copy-start.5 = (bf16[1552,256]{1,0:T(8,128)(2,1)}, bf16[1552,256]{1,0:T(8,128)(2,1)S(1)}, u32[]{:S(2)}) copy-start(bf16[1552,256]{1,0:T(8,128)(2,1)S(1)} %collective-permute-done.5.rest_2_) | copy-start | bytes 2383876
  48.6 34.6 %collective-permute-start.6 = (bf16[1552,256]{1,0:T(8,128)(2,1)S(1)}, bf16[1552,256]{1,0:T(8,128)(2,1)}, u32[]{:S(2)}, u32[]{:S(2)}) collective-permute-start(bf16[1552,256]{1,0:T(8,128)(2,1)S(1)} %collective-permute-done.5.rest_2_), channel_id=1, source_target_pairs={{0,1},{1,0},{2,3},{3,2},{4,5},{5,4},{6,7},{7,6},{8,9},{9,8},{10,11... | collective-permute-start | bytes 2383880 | tf_op jit(solution)/shard_map/ppermute | solution.py:337
  63.0 20.2 %collective-permute-start.8 = (bf16[1552,256]{1,0:T(8,128)(2,1)}, bf16[1552,256]{1,0:T(8,128)(2,1)}, u32[]{:S(2)}, u32[]{:S(2)}) collective-permute-start(bf16[1552,256]{1,0:T(8,128)(2,1)} %collective-permute-done.7.rest_4_), channel_id=1, source_target_pairs={{0,1},{1,0},{2,3},{3,2},{4,5},{5,4},{6,7},{7,6},{8,9},{9,8},{10,11... | collective-permute-start | bytes 2383880 | tf_op jit(solution)/shard_map/ppermute | solution.py:337
  65.0 6.4 %collective-permute-start = (bf16[2,32,256]{2,1,0:T(8,128)(2,1)S(1)}, bf16[2,32,256]{2,1,0:T(8,128)(2,1)S(1)}, u32[]{:S(2)}, u32[]{:S(2)}) collective-permute-start(bf16[2,32,256]{2,1,0:T(8,128)(2,1)S(1)} %get-tuple-element.7.carry), channel_id=1, source_target_pairs={{128,0},{384,256},{129,1},{385,257},{130,2},{386,258},{131,3},{387... | collective-permute-start | bytes 98312 | tf_op jit(solution)/shard_map/ppermute | solution.py:315
  66.3 8.4 %collective-permute-start.2 = (bf16[8,32,256]{2,1,0:T(8,128)(2,1)S(1)}, bf16[8,32,256]{2,1,0:T(8,128)(2,1)S(1)}, u32[]{:S(2)}, u32[]{:S(2)}) collective-permute-start(bf16[8,32,256]{2,1,0:T(8,128)(2,1)S(1)} %get-tuple-element.9), channel_id=1, source_target_pairs={{0,128},{128,256},{256,384},{1,129},{129,257},{257,385},{2,130},{1... | collective-permute-start | bytes 393224 | tf_op jit(solution)/shard_map/ppermute | solution.py:315
  71.4 9.5 %collective-permute-start.1 = (bf16[4,32,256]{2,1,0:T(8,128)(2,1)S(1)}, bf16[4,32,256]{2,1,0:T(8,128)(2,1)S(1)}, u32[]{:S(2)}, u32[]{:S(2)}) collective-permute-start(bf16[4,32,256]{2,1,0:T(8,128)(2,1)S(1)} %pad_maximum_fusion.1), channel_id=1, source_target_pairs={{256,0},{257,1},{258,2},{259,3},{260,4},{261,5},{262,6},{263,7},{2... | collective-permute-start | bytes 196616 | tf_op jit(solution)/shard_map/ppermute | solution.py:315
  75.3 17.6 %copy-start.1 = (bf16[24,32,256]{2,1,0:T(8,128)(2,1)}, bf16[24,32,256]{2,1,0:T(8,128)(2,1)S(1)}, u32[]{:S(2)}) copy-start(bf16[24,32,256]{2,1,0:T(8,128)(2,1)S(1)} %shard_map.70.mid) | copy-start | bytes 1179652
  75.3 12.6 %collective-permute-start.3 = (bf16[24,32,256]{2,1,0:T(8,128)(2,1)S(1)}, bf16[24,32,256]{2,1,0:T(8,128)(2,1)S(1)}, u32[]{:S(2)}, u32[]{:S(2)}) collective-permute-start(bf16[24,32,256]{2,1,0:T(8,128)(2,1)S(1)} %shard_map.70.mid), channel_id=1, source_target_pairs={{0,8},{8,16},{16,24},{24,32},{32,40},{40,48},{48,56},{56,64},{64,7... | collective-permute-start | bytes 1179656 | tf_op jit(solution)/shard_map/ppermute | solution.py:350
  80.9 12.0 %copy-start.10 = (bf16[4,32,256]{2,1,0:T(8,128)(2,1)}, bf16[4,32,256]{2,1,0:T(8,128)(2,1)S(1)}, u32[]{:S(2)}) copy-start(bf16[4,32,256]{2,1,0:T(8,128)(2,1)S(1)} %collective-permute-done.1.far) | copy-start | bytes 196612
  80.9 12.0 %collective-permute-start.4 = (bf16[24,32,256]{2,1,0:T(8,128)(2,1)S(1)}, bf16[24,32,256]{2,1,0:T(8,128)(2,1)S(1)}, u32[]{:S(2)}, u32[]{:S(2)}) collective-permute-start(bf16[24,32,256]{2,1,0:T(8,128)(2,1)S(1)} %shard_map.70.mid), channel_id=1, source_target_pairs={{8,0},{16,8},{24,16},{32,24},{40,32},{48,40},{56,48},{64,56},{72,6... | collective-permute-start | bytes 1179656 | tf_op jit(solution)/shard_map/ppermute | solution.py:351
  87.8 5.0 %copy-start.6 = (bf16[24,32,256]{2,1,0:T(8,128)(2,1)}, bf16[24,32,256]{2,1,0:T(8,128)(2,1)S(1)}, u32[]{:S(2)}) copy-start(bf16[24,32,256]{2,1,0:T(8,128)(2,1)S(1)} %collective-permute-done.3.left) | copy-start | bytes 1179652
  92.9 0.7 copy-start.7
  103.9 6.5 %collective-permute-start.11 = (bf16[4,32,256]{2,1,0:T(8,128)(2,1)S(1)}, bf16[4,32,256]{2,1,0:T(8,128)(2,1)S(1)}, u32[]{:S(2)}, u32[]{:S(2)}) collective-permute-start(bf16[4,32,256]{2,1,0:T(8,128)(2,1)S(1)} %bitcast.24), channel_id=1, source_target_pairs={{384,256},{385,257},{386,258},{387,259},{388,260},{389,261},{390,2... | collective-permute-start | bytes 196616 | tf_op jit(solution)/shard_map/ppermute | solution.py:315
  104.5 15.2 %collective-permute-start.13 = (bf16[20,32,256]{2,1,0:T(8,128)(2,1)}, bf16[20,32,256]{2,1,0:T(8,128)(2,1)S(1)}, u32[]{:S(2)}, u32[]{:S(2)}) collective-permute-start(bf16[20,32,256]{2,1,0:T(8,128)(2,1)} %get-tuple-element.11.mid), channel_id=1, source_target_pairs={{0,8},{8,16},{16,24},{24,32},{32,40},{40,48},{48,56},{56,64},{64,7... | collective-permute-start | bytes 983048 | tf_op jit(solution)/shard_map/ppermute | solution.py:350
  107.9 11.8 %collective-permute-start.14 = (bf16[20,32,256]{2,1,0:T(8,128)(2,1)}, bf16[20,32,256]{2,1,0:T(8,128)(2,1)S(1)}, u32[]{:S(2)}, u32[]{:S(2)}) collective-permute-start(bf16[20,32,256]{2,1,0:T(8,128)(2,1)} %get-tuple-element.11.mid), channel_id=1, source_target_pairs={{8,0},{16,8},{24,16},{32,24},{40,32},{48,40},{56,48},{64,56},{72,6... | collective-permute-start | bytes 983048 | tf_op jit(solution)/shard_map/ppermute | solution.py:351
  111.2 7.9 %collective-permute-start.12 = (bf16[2,32,256]{2,1,0:T(8,128)(2,1)S(1)}, bf16[2,32,256]{2,1,0:T(8,128)(2,1)S(1)}, u32[]{:S(2)}, u32[]{:S(2)}) collective-permute-start(bf16[2,32,256]{2,1,0:T(8,128)(2,1)S(1)} %slice_select_fusion), channel_id=1, source_target_pairs={{384,0},{256,128},{385,1},{257,129},{386,2},{258,130},{387,3},{259... | collective-permute-start | bytes 98312 | tf_op jit(solution)/shard_map/ppermute | solution.py:315
  119.7 0.7 copy-start.8
  120.5 0.7 copy-start.9
where the time goes:
time: 162 us; the launch traced here: 161 us
  starting transfers between devices  52.9 us (33%)
  waiting for transfers between devices  46.4 us (29%)
  blocking collectives  29.9 us (18%)
  Pallas kernels  22.1 us (14%)
  local copies, waits for them, and re-layouts  6.73 us (4%)
  other arithmetic  2.1 us (1%)
    ppermute x8, waiting for transfers between devices, over_segments(): return lax.ppermute(array, 'segment', pairs)  36.7 us
    all_to_all x1, blocking collectives, body(): sent = lax.all_to_all(out, 'shard', split_axis=0, concat_axis=0, tiled=True)  29.9 us
    ppermute x8, starting transfers between devices, over_segments(): return lax.ppermute(array, 'segment', pairs)  20.4 us
    pallas_call x2, Pallas kernels, pair_call(): call(functools.partial(pair_kernel, first), outs, [SMEM] + [VMEM] * 5 + [...  17.7 us
    all_to_all x1, starting transfers between devices, body(): lax.all_to_all(chunks, 'shard', split_axis=0, concat_axis=0, tiled=True)  15.2 us
    ppermute x2, starting transfers between devices, beside(): came_left = lax.ppermute(array, 'shard', up)  6.74 us
    ppermute x3, starting transfers between devices, body(): bufs += [buf, lax.ppermute(buf, 'stream', swap)]  5.73 us
    ppermute x2, waiting for transfers between devices, beside(): came_right = lax.ppermute(array, 'shard', down)  5 us
  transfers between devices with their start and end apart: 16, of which 9 were waited for; matrix products, arithmetic and copies ran while one was open for 1% of the time, Pallas kernels for 2%

commit v1 on v0

--- a/solution.py
+++ b/solution.py
@@ -20,7 +20,10 @@
 
 VMEM = pl.BlockSpec(memory_space=pltpu.VMEM)
 HBM = pl.BlockSpec(memory_space=pltpu.HBM)
-SMEM = pl.BlockSpec(memory_space=pltpu.SMEM)
+
+
+def core_of():
+    return lax.rem(lax.axis_index("stream"), 2)
 
 
 def shape_of(*dims, dtype=BF16):
@@ -51,8 +54,8 @@
                 out[z, at : at + 2, :] = row[frame, 2 * z : 2 * z + 2, lanes]
 
 
-def pack_kernel(scal, gain, taps_time, taps_space, out, sems):
-    at = pl.multiple_of(scal[1] * HALF, HALF)
+def pack_kernel(gain, taps_time, taps_space, out, sems):
+    at = pl.multiple_of(core_of() * HALF, HALF)
     copies = []
     for tap in range(TAPS):
         own = taps_time.at[0, tap] if tap < 3 else taps_space.at[0, tap - 3]
@@ -85,8 +88,8 @@
             carry[frame, col * 16 : col * 16 + 16, lanes] = got[:, 64 + 4 * side + n, :]
 
 
-def fetch(section, scal, own, bufs, out, terms, sems, gain_sem):
-    mine, core = scal[0], scal[1]
+def fetch(section, own, bufs, out, terms, sems, gain_sem):
+    mine, core = lax.axis_index("segment"), core_of()
     rel = lax.rem(section - mine + SECTIONS, SECTIONS)
     plan = []
     for tap in range(TAPS):
@@ -164,20 +167,21 @@
     return slice(col * 16, col * 16 + 16)
 
 
-def pair_kernel(first, scal, gain, far, mid, left, right, *rest):
-    if first:
-        refs, (out, tails) = rest[:8], rest[8:10]
+def pair_kernel(first, gain, far, wrapped, mid, left, right, *rest):
+    if first:
+        refs, (out, tails, tails_near) = rest[:8], rest[8:11]
     else:
         refs, (out,) = rest[:8], rest[8:9]
     own, bufs = refs[:2], refs[2:]
-    weights, terms, sems, gain_sem, normed, hidden, second, normed2 = rest[(10 if first else 9) :]
+    weights, terms, sems, gain_sem, normed, hidden, second, normed2 = rest[(11 if first else 9) :]
     section = 0 if first else 2
     total = 24 if first else 20
-    mine, shard, shards = scal[0], scal[2], scal[3]
+    mine, shard = lax.axis_index("segment"), lax.axis_index("shard")
+    shards = lax.axis_size("shard")
     loads = []
     for k in range(2):
         loads.append(
-            fetch(section + k, scal, own, bufs, weights.at[k], terms.at[k], sems.at[k], gain_sem.at[k])
+            fetch(section + k, own, bufs, weights.at[k], terms.at[k], sems.at[k], gain_sem.at[k])
         )
     if first:
         mine_rel = lax.rem(2 - mine + SECTIONS, SECTIONS)
@@ -196,7 +200,7 @@
             values = source[at : at + size].astype(F32).reshape(size * 32, C)
             normed[at : at + size, n * 32 : n * 32 + 32] = normed_of(values, row).reshape(size, 32, C)
     if first:
-        tails[0] = normed[total - 2 : total, 32:64]
+        tails[...] = normed[total - 2 : total, 32:64]
 
     @pl.when(mine == 0)
     def _():
@@ -222,7 +226,7 @@
         normed2[:, cols(col), :] = n.reshape(count, 16, C)
     own_tail = normed2[count - 2 : count, 16:48]
     if first:
-        tails[1] = own_tail
+        tails_near[0:2] = own_tail
 
     @pl.when(mine == 0)
     def _():
@@ -249,31 +253,32 @@
         received = rows[0:1] + (rows[1:2] + rows[2:3])
         row = jnp.where(mine == 2, gain[...], received)
         last = out[count - 2 : count].astype(F32).reshape(64, C)
-        tails[2] = normed_of(last, row).reshape(2, 32, C)
+        tails_near[2:4] = normed_of(last, row).reshape(2, 32, C)
 
         @pl.when(mine == 0)
         def _():
             out[0:4] = far[...]
 
     else:
-        carry = jnp.where(mine == SECTIONS - 1, own_tail, far[...])
+        carry = jnp.where(mine == 2, far[2:4], wrapped[...])
+        carry = jnp.where(mine == SECTIONS - 1, own_tail, carry)
         for side in range(2):
             lanes = slice(side * LANES, (side + 1) * LANES)
             for n in range(4):
                 out[:, 64 + 4 * side + n, :] = carry[n // 2, cols(n % 2), lanes]
 
 
-def pair_call(first, scal, gain, far, sources, own, bufs):
+def pair_call(first, gain, far, wrapped, sources, own, bufs):
     total = 24 if first else 20
     count = total - 2
     if first:
-        outs = (shape_of(20, 32, C), shape_of(3, 2, 32, C))
+        outs = (shape_of(20, 32, C), shape_of(2, 32, C), shape_of(4, 32, C))
     else:
         outs = shape_of(16, 72, LANES)
     return call(
         functools.partial(pair_kernel, first),
         outs,
-        [SMEM] + [VMEM] * 5 + [HBM] * 8,
+        [VMEM] * 6 + [HBM] * 8,
         [
             pltpu.VMEM((2, TAPS, C, C), BF16),
             pltpu.VMEM((3, 16, C), BF16),
@@ -286,27 +291,29 @@
         ],
         flops=1 << 31,
         moved=4 << 20,
-        room=58,
-    )(scal, gain, far, *sources, *own, *bufs)
-
-
-def join_kernel(scal, frames, before, near, carry, out):
+    )(gain, far, wrapped, *sources, *own, *bufs)
+
+
+def join_kernel(frames, before, near, carry, out, both):
     out[8:24] = frames[...]
     out[0:8] = before[...]
-
-    @pl.when(scal[0] == 0)
+    both[0:2] = near[...]
+    both[2:4] = carry[...]
+
+    @pl.when(lax.axis_index("segment") == 0)
     def _():
         out[4:6] = near[...]
         out[6:8] = carry[...]
+
+
+def choose_kernel(own, came, out):
+    out[...] = jnp.where(lax.axis_index("segment") == SECTIONS - 1, own[...], came[0:2])
 
 
 def body(latents, norm_gain, time_weight, space_weight, carry_in):
     shards = lax.axis_size("shard")
     streams = lax.axis_size("stream")
     mine = lax.axis_index("segment")
-    core = lax.rem(lax.axis_index("stream"), 2)
-    here = lax.axis_index("shard")
-    scal = jnp.stack([mine, core, here, jnp.int32(shards)]).astype(jnp.int32)
 
     def ring(distance):
         return [(i, (i + distance) % SECTIONS) for i in range(SECTIONS)]
@@ -327,10 +334,10 @@
     packed = call(
         pack_kernel,
         shape_of(PACKED, C),
-        [SMEM, VMEM, HBM, HBM],
+        [VMEM, HBM, HBM],
         [pltpu.SemaphoreType.DMA((TAPS,))],
         room=58,
-    )(scal, norm_gain, time_weight, space_weight)
+    )(norm_gain, time_weight, space_weight)
     bufs = []
     for distance in (-1, 2, 1):
         buf = over_segments(packed, ring(distance))
@@ -341,10 +348,10 @@
     )(got)
     before = over_segments(sent_before, [(0, 1), (1, 2), (2, 3)])
     near = over_segments(carry, [(1, 0), (3, 2)])
-    far = over_segments(jnp.concatenate([near, carry], axis=0), [(2, 0)])
-    joined = call(join_kernel, shape_of(24, 32, C), [SMEM] + [VMEM] * 4)(
-        scal, frames, before, near, carry
-    )
+    joined, both = call(join_kernel, (shape_of(24, 32, C), shape_of(4, 32, C)), [VMEM] * 4)(
+        frames, before, near, carry
+    )
+    far = over_segments(both, [(2, 0)])
 
     def beside(array):
         came_left = lax.ppermute(array, "shard", up)
@@ -352,12 +359,12 @@
         return array, came_left, came_right
 
     own = (time_weight, space_weight)
-    middle, tails = pair_call(True, scal, norm_gain, far, beside(joined), own, bufs)
+    middle, tail, tails_near = pair_call(True, norm_gain, far, carry, beside(joined), own, bufs)
     sources = beside(middle)
-    over = over_segments(tails[1:3].reshape(4, 32, C), [(3, 2)])
-    wrapped = over_segments(jnp.where(mine == 3, tails[0], over[0:2]), [(3, 0), (2, 1)])
-    carry = jnp.where(mine == 2, over[2:4], wrapped)
-    out = pair_call(False, scal, norm_gain, carry, sources, own, bufs)
+    over = over_segments(tails_near, [(3, 2)])
+    chosen = call(choose_kernel, shape_of(2, 32, C), [VMEM] * 2)(tail, over)
+    wrapped = over_segments(chosen, [(3, 0), (2, 1)])
+    out = pair_call(False, norm_gain, over, wrapped, sources, own, bufs)
     sent = lax.all_to_all(out, "shard", split_axis=0, concat_axis=0, tiled=True)
     main = jnp.concatenate([sent[:, 0:32], sent[:, 32:64]], axis=-1)
     decoded = main.reshape(32, 16, C).transpose(1, 0, 2)[None, None]

time: 162 us -> 155 us (0.957)
  the two profiles are of different devices: /device:TPU:32 before, /device:TPU:2 now
where the time goes in v1:
time: 155 us; the launch traced here: 154 us
  starting transfers between devices  52.1 us (34%)
  waiting for transfers between devices  49.1 us (32%)
  blocking collectives  29.2 us (19%)
  Pallas kernels  19 us (12%)
  local copies, waits for them, and re-layouts  3.66 us (2%)
    ppermute x8, waiting for transfers between devices, over_segments(): return lax.ppermute(array, 'segment', pairs)  42.7 us
    all_to_all x1, blocking collectives, body(): sent = lax.all_to_all(out, 'shard', split_axis=0, concat_axis=0, tiled=True)  29.2 us
    ppermute x8, starting transfers between devices, over_segments(): return lax.ppermute(array, 'segment', pairs)  19.4 us
    all_to_all x1, starting transfers between devices, body(): lax.all_to_all(chunks, 'shard', split_axis=0, concat_axis=0, tiled=True)  15.2 us
    pallas_call x2, Pallas kernels, pair_call(): call(functools.partial(pair_kernel, first), outs, [VMEM] * 6 + [HBM] * 8,...  15.2 us
    ppermute x2, starting transfers between devices, beside(): came_left = lax.ppermute(array, 'shard', up)  8.62 us
    ppermute x3, starting transfers between devices, body(): bufs += [buf, lax.ppermute(buf, 'stream', swap)]  6.23 us
    ppermute x2, waiting for transfers between devices, beside(): came_left = lax.ppermute(array, 'shard', up)  4.37 us
  transfers between devices with their start and end apart: 16, of which 7 were waited for; matrix products, arithmetic and copies ran while one was open for 0% of the time, Pallas kernels for 2%

profile of v1, /device:TPU:2, one launch (start us, length us, event | category | flops | bytes accessed | tf_op | source)
XLA Modules:
  0.0 154.0 jit_solution(897894548108729393)
XLA Ops:
  0.6 0.0 copy-start
  0.6 1.2 copy-done
  1.9 0.2 copy.13
  2.0 0.0 copy-start.3
  2.1 0.7 copy-done.3
  2.8 0.8 shard_map.68
  3.6 15.2 %all-to-all-start = ((bf16[16,72,128]{2,1,0:T(8,128)(2,1)}), bf16[16,72,128]{2,1,0:T(8,128)(2,1)S(1)}, u32[]{:S(2)}, u32[]{:S(2)}) async-start(bf16[16,72,128]{2,1,0:T(8,128)(2,1)} %shard_map.68), calls=%async_computation | async-start | bytes 589824 | tf_op jit(solution)/shard_map/all_to_all | solution.py:332
  18.8 0.0 copy-start.1
  18.8 0.0 copy-start.2
  18.8 0.0 copy-start.4
  18.8 3.0 %shard_map.71 = bf16[1552,256]{1,0:T(8,128)(2,1)} custom-call(f32[1,256]{1,0:T(1,128)} %gain.5, bf16[1,3,256,256]{3,2,1,0:T(8,128)(2,1)} %rest_0_.3, bf16[1,9,256,256]{3,2,1,0:T(8,128)(2,1)} %rest_1_.3), custom_call_target="tpu_custom_call" | custom-call | flops 1048576 | bytes 1048576 | tf_op jit(solution)/shard_map/pallas_call | solution.py:334
  21.8 3.5 %collective-permute-start.9 = (bf16[1552,256]{1,0:T(8,128)(2,1)}, bf16[1552,256]{1,0:T(8,128)(2,1)}, u32[]{:S(2)}, u32[]{:S(2)}) collective-permute-start(bf16[1552,256]{1,0:T(8,128)(2,1)} %shard_map.71), channel_id=1, source_target_pairs={{0,128},{128,256},{256,384},{384,0},{1,129},{129,257},{257,385},{3... | collective-permute-start | bytes 2383880 | tf_op jit(solution)/shard_map/ppermute | solution.py:322
  25.3 4.8 %collective-permute-start.7 = (bf16[1552,256]{1,0:T(8,128)(2,1)}, bf16[1552,256]{1,0:T(8,128)(2,1)}, u32[]{:S(2)}, u32[]{:S(2)}) collective-permute-start(bf16[1552,256]{1,0:T(8,128)(2,1)} %shard_map.71), channel_id=1, source_target_pairs={{0,256},{128,384},{256,0},{384,128},{1,257},{129,385},{257,1},{385... | collective-permute-start | bytes 2383880 | tf_op jit(solution)/shard_map/ppermute | solution.py:322
  30.1 3.3 %collective-permute-start.5 = (bf16[1552,256]{1,0:T(8,128)(2,1)}, bf16[1552,256]{1,0:T(8,128)(2,1)}, u32[]{:S(2)}, u32[]{:S(2)}) collective-permute-start(bf16[1552,256]{1,0:T(8,128)(2,1)} %shard_map.71), channel_id=1, source_target_pairs={{0,384},{128,0},{256,128},{384,256},{1,385},{129,1},{257,129},{385... | collective-permute-start | bytes 2383880 | tf_op jit(solution)/shard_map/ppermute | solution.py:322
  33.4 11.3 %collective-permute-done.9.rest_6_ = bf16[1552,256]{1,0:T(8,128)(2,1)} collective-permute-done((bf16[1552,256]{1,0:T(8,128)(2,1)}, bf16[1552,256]{1,0:T(8,128)(2,1)}, u32[]{:S(2)}, u32[]{:S(2)}) %collective-permute-start.9) | collective-permute-done | bytes 794656 | tf_op jit(solution)/shard_map/ppermute | solution.py:322
  44.7 1.9 %collective-permute-start.10 = (bf16[1552,256]{1,0:T(8,128)(2,1)}, bf16[1552,256]{1,0:T(8,128)(2,1)}, u32[]{:S(2)}, u32[]{:S(2)}) collective-permute-start(bf16[1552,256]{1,0:T(8,128)(2,1)} %collective-permute-done.9.rest_6_), channel_id=1, source_target_pairs={{0,1},{1,0},{2,3},{3,2},{4,5},{5,4},{6,7},{7,6},{8,9},{9,8},{10,11... | collective-permute-start | bytes 2383880 | tf_op jit(solution)/shard_map/ppermute | solution.py:344
  46.6 16.0 %collective-permute-done.7.rest_4_ = bf16[1552,256]{1,0:T(8,128)(2,1)} collective-permute-done((bf16[1552,256]{1,0:T(8,128)(2,1)}, bf16[1552,256]{1,0:T(8,128)(2,1)}, u32[]{:S(2)}, u32[]{:S(2)}) %collective-permute-start.7) | collective-permute-done | bytes 794656 | tf_op jit(solution)/shard_map/ppermute | solution.py:322
  62.6 1.9 %collective-permute-start.8 = (bf16[1552,256]{1,0:T(8,128)(2,1)}, bf16[1552,256]{1,0:T(8,128)(2,1)}, u32[]{:S(2)}, u32[]{:S(2)}) collective-permute-start(bf16[1552,256]{1,0:T(8,128)(2,1)} %collective-permute-done.7.rest_4_), channel_id=1, source_target_pairs={{0,1},{1,0},{2,3},{3,2},{4,5},{5,4},{6,7},{7,6},{8,9},{9,8},{10,11... | collective-permute-start | bytes 2383880 | tf_op jit(solution)/shard_map/ppermute | solution.py:344
  64.6 0.0 collective-permute-done.5.rest_2_
  64.6 2.4 %collective-permute-start.6 = (bf16[1552,256]{1,0:T(8,128)(2,1)}, bf16[1552,256]{1,0:T(8,128)(2,1)}, u32[]{:S(2)}, u32[]{:S(2)}) collective-permute-start(bf16[1552,256]{1,0:T(8,128)(2,1)} %collective-permute-done.5.rest_2_), channel_id=1, source_target_pairs={{0,1},{1,0},{2,3},{3,2},{4,5},{5,4},{6,7},{7,6},{8,9},{9,8},{10,11... | collective-permute-start | bytes 2383880 | tf_op jit(solution)/shard_map/ppermute | solution.py:344
  67.0 0.0 all-to-all-done.got
  67.0 0.1 shard_map.69
  67.1 3.3 %collective-permute-start = (bf16[8,32,256]{2,1,0:T(8,128)(2,1)S(1)}, bf16[8,32,256]{2,1,0:T(8,128)(2,1)S(1)}, u32[]{:S(2)}, u32[]{:S(2)}) collective-permute-start(bf16[8,32,256]{2,1,0:T(8,128)(2,1)S(1)} %get-tuple-element.11), channel_id=1, source_target_pairs={{0,128},{128,256},{256,384},{1,129},{129,257},{257,385},{2,130},{1... | collective-permute-start | bytes 393224 | tf_op jit(solution)/shard_map/ppermute | solution.py:322
  70.4 1.3 collective-permute-start.1
  71.7 4.5 %collective-permute-done.1.near = bf16[2,32,256]{2,1,0:T(8,128)(2,1)S(1)} collective-permute-done((bf16[2,32,256]{2,1,0:T(8,128)(2,1)S(1)}, bf16[2,32,256]{2,1,0:T(8,128)(2,1)S(1)}, u32[]{:S(2)}, u32[]{:S(2)}) %collective-permute-start.1) | collective-permute-done | bytes 32800 | tf_op jit(solution)/shard_map/ppermute | solution.py:322
  76.2 0.0 collective-permute-done.before
  76.3 1.3 collective-permute-start.2
  77.6 1.3 collective-permute-start.4
  78.9 5.1 %collective-permute-done.2.far = bf16[4,32,256]{2,1,0:T(8,128)(2,1)S(1)} collective-permute-done((bf16[4,32,256]{2,1,0:T(8,128)(2,1)S(1)}, bf16[4,32,256]{2,1,0:T(8,128)(2,1)S(1)}, u32[]{:S(2)}, u32[]{:S(2)}) %collective-permute-start.2) | collective-permute-done | bytes 65568 | tf_op jit(solution)/shard_map/ppermute | solution.py:322
  84.0 3.6 %collective-permute-start.3 = (bf16[24,32,256]{2,1,0:T(8,128)(2,1)S(1)}, bf16[24,32,256]{2,1,0:T(8,128)(2,1)S(1)}, u32[]{:S(2)}, u32[]{:S(2)}) collective-permute-start(bf16[24,32,256]{2,1,0:T(8,128)(2,1)S(1)} %get-tuple-element.14.mid), channel_id=1, source_target_pairs={{0,8},{8,16},{16,24},{24,32},{32,40},{40,48},{48,56},{56,64},{64,7... | collective-permute-start | bytes 1179656 | tf_op jit(solution)/shard_map/ppermute | solution.py:357
  87.5 0.0 collective-permute-done.10.rest_7_
  87.5 0.0 collective-permute-done.8.rest_5_
  87.5 0.0 collective-permute-done.6.rest_3_
  87.6 2.0 %collective-permute-done.4.right = bf16[24,32,256]{2,1,0:T(8,128)(2,1)S(1)} collective-permute-done((bf16[24,32,256]{2,1,0:T(8,128)(2,1)S(1)}, bf16[24,32,256]{2,1,0:T(8,128)(2,1)S(1)}, u32[]{:S(2)}, u32[]{:S(2)}) %collective-permute-start.4) | collective-permute-done | bytes 393248 | tf_op jit(solution)/shard_map/ppermute | solution.py:358
  89.6 4.4 %collective-permute-done.3.left = bf16[24,32,256]{2,1,0:T(8,128)(2,1)S(1)} collective-permute-done((bf16[24,32,256]{2,1,0:T(8,128)(2,1)S(1)}, bf16[24,32,256]{2,1,0:T(8,128)(2,1)S(1)}, u32[]{:S(2)}, u32[]{:S(2)}) %collective-permute-start.3) | collective-permute-done | bytes 393248 | tf_op jit(solution)/shard_map/ppermute | solution.py:357
  93.9 8.8 %shard_map.72 = (bf16[20,32,256]{2,1,0:T(8,128)(2,1)S(1)}, bf16[2,32,256]{2,1,0:T(8,128)(2,1)S(1)}, bf16[4,32,256]{2,1,0:T(8,128)(2,1)S(1)}) custom-call(f32[1,256]{1,0:T(1,128)S(1)} %copy-done.4, bf16[4,32,256]{2,1,0:T(8,128)(2,1)S(1)} %collective-permute-done.2.far, bf16[2,32,256]{2,1,0:T(8,128)(2,1)S(1)} %get-tuple-element.12.carry.wrapped, ...), custom_call_target="tpu_custom_call" | custom-call | flops 2147483648 | bytes 4194304 | tf_op jit(solution)/shard_map/pallas_call | solution.py:278
  102.8 1.3 collective-permute-start.14
  104.1 5.1 %collective-permute-start.13 = (bf16[20,32,256]{2,1,0:T(8,128)(2,1)S(1)}, bf16[20,32,256]{2,1,0:T(8,128)(2,1)S(1)}, u32[]{:S(2)}, u32[]{:S(2)}) collective-permute-start(bf16[20,32,256]{2,1,0:T(8,128)(2,1)S(1)} %get-tuple-element.17.mid), channel_id=1, source_target_pairs={{0,8},{8,16},{16,24},{24,32},{32,40},{40,48},{48,56},{56,64},{64,7... | collective-permute-start | bytes 983048 | tf_op jit(solution)/shard_map/ppermute | solution.py:357
  109.1 0.7 collective-permute-start.11
  109.8 0.0 collective-permute-done.11.came.far
  109.9 1.3 collective-permute-start.12
  111.2 5.7 %collective-permute-done.12.wrapped = bf16[2,32,256]{2,1,0:T(8,128)(2,1)S(1)} collective-permute-done((bf16[2,32,256]{2,1,0:T(8,128)(2,1)S(1)}, bf16[2,32,256]{2,1,0:T(8,128)(2,1)S(1)}, u32[]{:S(2)}, u32[]{:S(2)}) %collective-permute-start.12) | collective-permute-done | bytes 32800 | tf_op jit(solution)/shard_map/ppermute | solution.py:322
  116.9 0.0 collective-permute-done.14.right
  116.9 0.0 collective-permute-done.13.left
  116.9 6.4 %shard_map.74 = bf16[16,72,128]{2,1,0:T(8,128)(2,1)S(1)} custom-call(f32[1,256]{1,0:T(1,128)S(1)} %copy-done.4, bf16[4,32,256]{2,1,0:T(8,128)(2,1)S(1)} %collective-permute-done.11.came.far, bf16[2,32,256]{2,1,0:T(8,128)(2,1)S(1)} %collective-permute-done.12.wrapped, bf16[20,32,256]{2,1,0:T(8,128)(2,1)S(1)} %get-tuple-element.17.mid, ...), custom_call_target="tpu_custom_call" | custom-call | flops 2147483648 | bytes 4194304 | tf_op jit(solution)/shard_map/pallas_call | solution.py:278
  123.2 29.2 %all_to_all.10 = bf16[16,72,128]{2,1,0:T(8,128)(2,1)S(1)} all-to-all(bf16[16,72,128]{2,1,0:T(8,128)(2,1)S(1)} %shard_map.74), channel_id=1, replica_groups=mesh['segment'=4,'shard'=16,'stream'=8] {'shard'}, dimensions={0} | all-to-all | bytes 589824 | tf_op jit(solution)/shard_map/all_to_all | solution.py:368
  152.5 0.8 copy.12
  153.3 0.6 reshape.16
  (12 shorter events, 0.2 us)
Async XLA Ops:
  0.6 1.2 copy-start
  2.0 0.8 copy-start.3
  3.6 63.4 %all-to-all-start = ((bf16[16,72,128]{2,1,0:T(8,128)(2,1)}), bf16[16,72,128]{2,1,0:T(8,128)(2,1)S(1)}, u32[]{:S(2)}, u32[]{:S(2)}) async-start(bf16[16,72,128]{2,1,0:T(8,128)(2,1)} %shard_map.68), calls=%async_computation | async-start | bytes 589824 | tf_op jit(solution)/shard_map/all_to_all | solution.py:332
  18.8 75.2 %copy-start.1 = (bf16[1,9,256,256]{3,2,1,0:T(8,128)(2,1)S(1)}, bf16[1,9,256,256]{3,2,1,0:T(8,128)(2,1)}, u32[]{:S(2)}) copy-start(bf16[1,9,256,256]{3,2,1,0:T(8,128)(2,1)} %rest_1_.3) | copy-start | bytes 3538948
  18.8 75.1 %copy-start.2 = (bf16[1,3,256,256]{3,2,1,0:T(8,128)(2,1)S(1)}, bf16[1,3,256,256]{3,2,1,0:T(8,128)(2,1)}, u32[]{:S(2)}) copy-start(bf16[1,3,256,256]{3,2,1,0:T(8,128)(2,1)} %rest_0_.3) | copy-start | bytes 1179652
  18.8 75.1 %copy-start.4 = (f32[1,256]{1,0:T(1,128)S(1)}, f32[1,256]{1,0:T(1,128)}, u32[]{:S(2)}) copy-start(f32[1,256]{1,0:T(1,128)} %gain.5) | copy-start | bytes 3076
  21.8 22.9 %collective-permute-start.9 = (bf16[1552,256]{1,0:T(8,128)(2,1)}, bf16[1552,256]{1,0:T(8,128)(2,1)}, u32[]{:S(2)}, u32[]{:S(2)}) collective-permute-start(bf16[1552,256]{1,0:T(8,128)(2,1)} %shard_map.71), channel_id=1, source_target_pairs={{0,128},{128,256},{256,384},{384,0},{1,129},{129,257},{257,385},{3... | collective-permute-start | bytes 2383880 | tf_op jit(solution)/shard_map/ppermute | solution.py:322
  25.3 37.4 %collective-permute-start.7 = (bf16[1552,256]{1,0:T(8,128)(2,1)}, bf16[1552,256]{1,0:T(8,128)(2,1)}, u32[]{:S(2)}, u32[]{:S(2)}) collective-permute-start(bf16[1552,256]{1,0:T(8,128)(2,1)} %shard_map.71), channel_id=1, source_target_pairs={{0,256},{128,384},{256,0},{384,128},{1,257},{129,385},{257,1},{385... | collective-permute-start | bytes 2383880 | tf_op jit(solution)/shard_map/ppermute | solution.py:322
  30.1 34.5 %collective-permute-start.5 = (bf16[1552,256]{1,0:T(8,128)(2,1)}, bf16[1552,256]{1,0:T(8,128)(2,1)}, u32[]{:S(2)}, u32[]{:S(2)}) collective-permute-start(bf16[1552,256]{1,0:T(8,128)(2,1)} %shard_map.71), channel_id=1, source_target_pairs={{0,384},{128,0},{256,128},{384,256},{1,385},{129,1},{257,129},{385... | collective-permute-start | bytes 2383880 | tf_op jit(solution)/shard_map/ppermute | solution.py:322
  44.7 42.8 %collective-permute-start.10 = (bf16[1552,256]{1,0:T(8,128)(2,1)}, bf16[1552,256]{1,0:T(8,128)(2,1)}, u32[]{:S(2)}, u32[]{:S(2)}) collective-permute-start(bf16[1552,256]{1,0:T(8,128)(2,1)} %collective-permute-done.9.rest_6_), channel_id=1, source_target_pairs={{0,1},{1,0},{2,3},{3,2},{4,5},{5,4},{6,7},{7,6},{8,9},{9,8},{10,11... | collective-permute-start | bytes 2383880 | tf_op jit(solution)/shard_map/ppermute | solution.py:344
  62.6 24.9 %collective-permute-start.8 = (bf16[1552,256]{1,0:T(8,128)(2,1)}, bf16[1552,256]{1,0:T(8,128)(2,1)}, u32[]{:S(2)}, u32[]{:S(2)}) collective-permute-start(bf16[1552,256]{1,0:T(8,128)(2,1)} %collective-permute-done.7.rest_4_), channel_id=1, source_target_pairs={{0,1},{1,0},{2,3},{3,2},{4,5},{5,4},{6,7},{7,6},{8,9},{9,8},{10,11... | collective-permute-start | bytes 2383880 | tf_op jit(solution)/shard_map/ppermute | solution.py:344
  64.6 23.0 %collective-permute-start.6 = (bf16[1552,256]{1,0:T(8,128)(2,1)}, bf16[1552,256]{1,0:T(8,128)(2,1)}, u32[]{:S(2)}, u32[]{:S(2)}) collective-permute-start(bf16[1552,256]{1,0:T(8,128)(2,1)} %collective-permute-done.5.rest_2_), channel_id=1, source_target_pairs={{0,1},{1,0},{2,3},{3,2},{4,5},{5,4},{6,7},{7,6},{8,9},{9,8},{10,11... | collective-permute-start | bytes 2383880 | tf_op jit(solution)/shard_map/ppermute | solution.py:344
  67.1 9.2 %collective-permute-start = (bf16[8,32,256]{2,1,0:T(8,128)(2,1)S(1)}, bf16[8,32,256]{2,1,0:T(8,128)(2,1)S(1)}, u32[]{:S(2)}, u32[]{:S(2)}) collective-permute-start(bf16[8,32,256]{2,1,0:T(8,128)(2,1)S(1)} %get-tuple-element.11), channel_id=1, source_target_pairs={{0,128},{128,256},{256,384},{1,129},{129,257},{257,385},{2,130},{1... | collective-permute-start | bytes 393224 | tf_op jit(solution)/shard_map/ppermute | solution.py:322
  70.4 5.8 %collective-permute-start.1 = (bf16[2,32,256]{2,1,0:T(8,128)(2,1)S(1)}, bf16[2,32,256]{2,1,0:T(8,128)(2,1)S(1)}, u32[]{:S(2)}, u32[]{:S(2)}) collective-permute-start(bf16[2,32,256]{2,1,0:T(8,128)(2,1)S(1)} %get-tuple-element.12.carry.wrapped), channel_id=1, source_target_pairs={{128,0},{384,256},{129,1},{385,257},{130,2},{386,258},{131,3},{387... | collective-permute-start | bytes 98312 | tf_op jit(solution)/shard_map/ppermute | solution.py:322
  76.3 7.7 %collective-permute-start.2 = (bf16[4,32,256]{2,1,0:T(8,128)(2,1)S(1)}, bf16[4,32,256]{2,1,0:T(8,128)(2,1)S(1)}, u32[]{:S(2)}, u32[]{:S(2)}) collective-permute-start(bf16[4,32,256]{2,1,0:T(8,128)(2,1)S(1)} %get-tuple-element.13), channel_id=1, source_target_pairs={{256,0},{257,1},{258,2},{259,3},{260,4},{261,5},{262,6},{263,7},{2... | collective-permute-start | bytes 196616 | tf_op jit(solution)/shard_map/ppermute | solution.py:322
  77.6 12.0 %collective-permute-start.4 = (bf16[24,32,256]{2,1,0:T(8,128)(2,1)S(1)}, bf16[24,32,256]{2,1,0:T(8,128)(2,1)S(1)}, u32[]{:S(2)}, u32[]{:S(2)}) collective-permute-start(bf16[24,32,256]{2,1,0:T(8,128)(2,1)S(1)} %get-tuple-element.14.mid), channel_id=1, source_target_pairs={{8,0},{16,8},{24,16},{32,24},{40,32},{48,40},{56,48},{64,56},{72,6... | collective-permute-start | bytes 1179656 | tf_op jit(solution)/shard_map/ppermute | solution.py:358
  84.0 10.0 %collective-permute-start.3 = (bf16[24,32,256]{2,1,0:T(8,128)(2,1)S(1)}, bf16[24,32,256]{2,1,0:T(8,128)(2,1)S(1)}, u32[]{:S(2)}, u32[]{:S(2)}) collective-permute-start(bf16[24,32,256]{2,1,0:T(8,128)(2,1)S(1)} %get-tuple-element.14.mid), channel_id=1, source_target_pairs={{0,8},{8,16},{16,24},{24,32},{32,40},{40,48},{48,56},{56,64},{64,7... | collective-permute-start | bytes 1179656 | tf_op jit(solution)/shard_map/ppermute | solution.py:357
  102.8 14.1 %collective-permute-start.14 = (bf16[20,32,256]{2,1,0:T(8,128)(2,1)S(1)}, bf16[20,32,256]{2,1,0:T(8,128)(2,1)S(1)}, u32[]{:S(2)}, u32[]{:S(2)}) collective-permute-start(bf16[20,32,256]{2,1,0:T(8,128)(2,1)S(1)} %get-tuple-element.17.mid), channel_id=1, source_target_pairs={{8,0},{16,8},{24,16},{32,24},{40,32},{48,40},{56,48},{64,56},{72,6... | collective-permute-start | bytes 983048 | tf_op jit(solution)/shard_map/ppermute | solution.py:358
  104.1 12.8 %collective-permute-start.13 = (bf16[20,32,256]{2,1,0:T(8,128)(2,1)S(1)}, bf16[20,32,256]{2,1,0:T(8,128)(2,1)S(1)}, u32[]{:S(2)}, u32[]{:S(2)}) collective-permute-start(bf16[20,32,256]{2,1,0:T(8,128)(2,1)S(1)} %get-tuple-element.17.mid), channel_id=1, source_target_pairs={{0,8},{8,16},{16,24},{24,32},{32,40},{40,48},{48,56},{56,64},{64,7... | collective-permute-start | bytes 983048 | tf_op jit(solution)/shard_map/ppermute | solution.py:357
  109.1 0.7 collective-permute-start.11
  109.9 7.0 %collective-permute-start.12 = (bf16[2,32,256]{2,1,0:T(8,128)(2,1)S(1)}, bf16[2,32,256]{2,1,0:T(8,128)(2,1)S(1)}, u32[]{:S(2)}, u32[]{:S(2)}) collective-permute-start(bf16[2,32,256]{2,1,0:T(8,128)(2,1)S(1)} %shard_map.73), channel_id=1, source_target_pairs={{384,0},{256,128},{385,1},{257,129},{386,2},{258,130},{387,3},{259... | collective-permute-start | bytes 98312 | tf_op jit(solution)/shard_map/ppermute | solution.py:322

commit v2 on v1

--- a/solution.py
+++ b/solution.py
@@ -88,46 +88,58 @@
             carry[frame, col * 16 : col * 16 + 16, lanes] = got[:, 64 + 4 * side + n, :]
 
 
-def fetch(section, own, bufs, out, terms, sems, gain_sem):
-    mine, core = lax.axis_index("segment"), core_of()
-    rel = lax.rem(section - mine + SECTIONS, SECTIONS)
-    plan = []
-    for tap in range(TAPS):
-        for side in range(2):
-            at = pl.multiple_of((core if side == 0 else 1 - core) * HALF, HALF)
-            plan.append((tap, side, at, out.at[tap, pl.ds(at, HALF)]))
-    taps_time, taps_space = own
-
-    @pl.when(rel == 0)
-    def _():
-        for tap, side, at, dst in plan:
-            src = taps_time.at[0, tap] if tap < 3 else taps_space.at[0, tap - 3]
-            pltpu.make_async_copy(src.at[pl.ds(at, HALF)], dst, sems.at[tap, side]).start()
-        pltpu.make_async_copy(bufs[0].at[pl.ds(GAIN_ROW, 16)], terms, gain_sem).start()
-
-    for which in range(3):
-
-        @pl.when(rel == which + 1)
-        def _(which=which):
-            for tap, side, at, dst in plan:
-                src = bufs[2 * which + side].at[pl.ds(tap * HALF, HALF)]
-                pltpu.make_async_copy(src, dst, sems.at[tap, side]).start()
-            pltpu.make_async_copy(bufs[2 * which].at[pl.ds(GAIN_ROW, 16)], terms, gain_sem).start()
-
-    def wait(first, last):
-        for tap, side, at, dst in plan:
-            if first <= tap < last:
-                pltpu.make_async_copy(
-                    bufs[side].at[pl.ds(tap * HALF, HALF)], dst, sems.at[tap, side]
-                ).wait()
-
-    def gain_row(gain):
-        pltpu.make_async_copy(bufs[0].at[pl.ds(GAIN_ROW, 16)], terms, gain_sem).wait()
+def stack_kernel(*refs):
+    bufs, out, sems = refs[:SECTIONS], refs[SECTIONS], refs[SECTIONS + 1]
+    copies = []
+    for which, buf in enumerate(bufs):
+        to = out.at[pl.ds(which * PACKED, PACKED)]
+        copies.append(pltpu.make_async_copy(buf, to, sems.at[which]))
+        copies[-1].start()
+    for copy in copies:
+        copy.wait()
+
+
+GROUPS = ((0, 3), (3, TAPS))
+
+
+def base_of(section):
+    rel = lax.rem(section - lax.axis_index("segment") + SECTIONS, SECTIONS)
+    return pl.multiple_of(rel * PACKED, 16)
+
+
+def fetch(section, bufs, out, terms, sems, gain_sem):
+    core = core_of()
+    base = base_of(section)
+    gain_copy = pltpu.make_async_copy(bufs[0].at[pl.ds(base + GAIN_ROW, 16)], terms, gain_sem)
+    gain_copy.start()
+    copies = []
+    for first, last in GROUPS:
+        at, size = first * HALF, (last - first) * HALF
+        for part in range(2):
+            side = core if part == 0 else 1 - core
+            src = bufs[part].at[pl.ds(pl.multiple_of(base + at, 16), size)]
+            copies.append(
+                pltpu.make_async_copy(src, out.at[side, pl.ds(at, size)], sems.at[len(copies)])
+            )
+            copies[-1].start()
+
+    def wait(group):
+        copies[2 * group].wait()
+        copies[2 * group + 1].wait()
+
+    def gain_row():
+        gain_copy.wait()
         rows = terms[...].astype(F32)
-        received = rows[0:1] + (rows[1:2] + rows[2:3])
-        return jnp.where(rel == 0, gain[...], received)
+        return rows[0:1] + (rows[1:2] + rows[2:3])
 
     return wait, gain_row
+
+
+def times_taps(parts, weights, tap):
+    rows = slice(tap * HALF, (tap + 3) * HALF)
+    lhs = [part[:, side * HALF : (side + 1) * HALF] for side in range(2) for part in parts]
+    taps = jnp.concatenate([weights[0, rows], weights[1, rows]], axis=0)
+    return jnp.dot(jnp.concatenate(lhs, axis=-1), taps, preferred_element_type=F32)
 
 
 def normed_of(values, gain_row):
@@ -140,11 +152,10 @@
 
 
 def mix(source, weights, hidden, count, columns):
-    taps = weights[0:3].reshape(3 * C, C)
     rows = columns * 16
     for at, size in pieces(count, 4):
         parts = [source[at + k : at + k + size, 0:rows].reshape(size * rows, C) for k in range(3)]
-        mixed = jnp.dot(jnp.concatenate(parts, axis=-1), taps, preferred_element_type=F32)
+        mixed = times_taps(parts, weights, 0)
         value = jax.nn.silu(mixed).astype(BF16).reshape(size, rows, C)
         for col in range(columns):
             hidden[col, at : at + size] = value[:, col * 16 : col * 16 + 16, :]
@@ -153,11 +164,8 @@
 def spatial(hidden, weights, col, count):
     size = count * 16
     row = lax.broadcasted_iota(jnp.int32, (size, C), 0) % 16
-    lhs = jnp.concatenate([hidden[col + q, 0:count].reshape(size, C) for q in range(3)], axis=-1)
-    y = []
-    for p in range(3):
-        taps = weights[3 + 3 * p : 6 + 3 * p].reshape(3 * C, C)
-        y.append(jnp.dot(lhs, taps, preferred_element_type=F32))
+    parts = [hidden[col + q, 0:count].reshape(size, C) for q in range(3)]
+    y = [times_taps(parts, weights, 3 + 3 * p) for p in range(3)]
     down = jnp.where(row == 0, 0.0, pltpu.roll(y[0], 1, 0))
     up = jnp.where(row == 15, 0.0, pltpu.roll(y[2], size - 1, 0))
     return y[1] + down + up
@@ -167,13 +175,13 @@
     return slice(col * 16, col * 16 + 16)
 
 
-def pair_kernel(first, gain, far, wrapped, mid, left, right, *rest):
-    if first:
-        refs, (out, tails, tails_near) = rest[:8], rest[8:11]
+def pair_kernel(first, far, wrapped, mid, left, right, stacked, swapped, *rest):
+    if first:
+        out, tails, tails_near = rest[:3]
     else:
-        refs, (out,) = rest[:8], rest[8:9]
-    own, bufs = refs[:2], refs[2:]
-    weights, terms, sems, gain_sem, normed, hidden, second, normed2 = rest[(11 if first else 9) :]
+        (out,) = rest[:1]
+    weights, terms, sems, gain_sem, normed, hidden, second, normed2 = rest[-8:]
+    bufs = (stacked, swapped)
     section = 0 if first else 2
     total = 24 if first else 20
     mine, shard = lax.axis_index("segment"), lax.axis_index("shard")
@@ -181,19 +189,14 @@
     loads = []
     for k in range(2):
         loads.append(
-            fetch(section + k, own, bufs, weights.at[k], terms.at[k], sems.at[k], gain_sem.at[k])
+            fetch(section + k, bufs, weights.at[k], terms.at[k], sems.at[k], gain_sem.at[k])
         )
-    if first:
-        mine_rel = lax.rem(2 - mine + SECTIONS, SECTIONS)
-        for which in range(3):
-
-            @pl.when(lax.rem(mine_rel + 2, 3) == which)
-            def _(which=which):
-                pltpu.make_async_copy(
-                    bufs[2 * which].at[pl.ds(GAIN_ROW, 16)], terms.at[2], gain_sem.at[2]
-                ).start()
-
-    row = loads[0][1](gain)
+    last_gain = pltpu.make_async_copy(
+        stacked.at[pl.ds(base_of(2) + GAIN_ROW, 16)], terms.at[2], gain_sem.at[2]
+    )
+    if first:
+        last_gain.start()
+    row = loads[0][1]()
     sources = (left, mid, right)
     for n, source in enumerate(sources):
         for at, size in pieces(total, 8):
@@ -207,11 +210,11 @@
         for n, source in enumerate(sources):
             normed[total - 18 : total - 16, n * 32 : n * 32 + 32] = source[total - 18 : total - 16]
 
-    loads[0][0](0, 3)
+    loads[0][0](0)
     count = total - 2
     mix(normed, weights.at[0], hidden, count, 6)
-    loads[0][0](3, TAPS)
-    row = loads[1][1](gain)
+    loads[0][0](1)
+    row = loads[1][1]()
     for col in range(4):
         source, at = ((left, cols(1)), (mid, cols(0)), (mid, cols(1)), (right, cols(0)))[col]
         a = source[2:, at, :].reshape(count * 16, C).astype(F32)
@@ -234,10 +237,10 @@
             source, at = ((left, cols(1)), (mid, cols(0)), (mid, cols(1)), (right, cols(0)))[col]
             normed2[count - 18 : count - 16, cols(col)] = source[total - 20 : total - 18, at, :]
 
-    loads[1][0](0, 3)
+    loads[1][0](0)
     count = total - 4
     mix(normed2, weights.at[1], hidden, count, 4)
-    loads[1][0](3, TAPS)
+    loads[1][0](1)
     for col in range(2):
         a = second[2:, cols(col), :].reshape(count * 16, C).astype(F32)
         result = (a + spatial(hidden, weights.at[1], col, count)).astype(BF16).reshape(count, 16, C)
@@ -248,10 +251,9 @@
                 lanes = slice(side * LANES, (side + 1) * LANES)
                 out[:, side * 32 + col * 16 : side * 32 + col * 16 + 16, :] = result[:, :, lanes]
     if first:
-        pltpu.make_async_copy(bufs[0].at[pl.ds(GAIN_ROW, 16)], terms.at[2], gain_sem.at[2]).wait()
+        last_gain.wait()
         rows = terms[2].astype(F32)
-        received = rows[0:1] + (rows[1:2] + rows[2:3])
-        row = jnp.where(mine == 2, gain[...], received)
+        row = rows[0:1] + (rows[1:2] + rows[2:3])
         last = out[count - 2 : count].astype(F32).reshape(64, C)
         tails_near[2:4] = normed_of(last, row).reshape(2, 32, C)
 
@@ -268,7 +270,7 @@
                 out[:, 64 + 4 * side + n, :] = carry[n // 2, cols(n % 2), lanes]
 
 
-def pair_call(first, gain, far, wrapped, sources, own, bufs):
+def pair_call(first, far, wrapped, sources, bufs):
     total = 24 if first else 20
     count = total - 2
     if first:
@@ -278,11 +280,11 @@
     return call(
         functools.partial(pair_kernel, first),
         outs,
-        [VMEM] * 6 + [HBM] * 8,
+        [VMEM] * 5 + [HBM] * 2,
         [
-            pltpu.VMEM((2, TAPS, C, C), BF16),
+            pltpu.VMEM((2, 2, GAIN_ROW, C), BF16),
             pltpu.VMEM((3, 16, C), BF16),
-            pltpu.SemaphoreType.DMA((2, TAPS, 2)),
+            pltpu.SemaphoreType.DMA((2, 4)),
             pltpu.SemaphoreType.DMA((3,)),
             pltpu.VMEM((total, 96, C), BF16),
             pltpu.VMEM((6, count, 16, C), BF16),
@@ -291,7 +293,7 @@
         ],
         flops=1 << 31,
         moved=4 << 20,
-    )(gain, far, wrapped, *sources, *own, *bufs)
+    )(far, wrapped, *sources, *bufs)
 
 
 def join_kernel(frames, before, near, carry, out, both):
@@ -338,10 +340,16 @@
         [pltpu.SemaphoreType.DMA((TAPS,))],
         room=58,
     )(norm_gain, time_weight, space_weight)
-    bufs = []
+    halves = [packed]
     for distance in (-1, 2, 1):
-        buf = over_segments(packed, ring(distance))
-        bufs += [buf, lax.ppermute(buf, "stream", swap)]
+        halves.append(over_segments(packed, ring(distance)))
+    stacked = call(
+        stack_kernel,
+        shape_of(SECTIONS * PACKED, C),
+        [HBM] * SECTIONS,
+        [pltpu.SemaphoreType.DMA((SECTIONS,))],
+    )(*halves)
+    bufs = (stacked, lax.ppermute(stacked, "stream", swap))
 
     frames, sent_before, carry = call(
         unpack_kernel, (shape_of(16, 32, C), shape_of(8, 32, C), shape_of(2, 32, C)), [VMEM]
@@ -358,13 +366,12 @@
         came_right = lax.ppermute(array, "shard", down)
         return array, came_left, came_right
 
-    own = (time_weight, space_weight)
-    middle, tail, tails_near = pair_call(True, norm_gain, far, carry, beside(joined), own, bufs)
+    middle, tail, tails_near = pair_call(True, far, carry, beside(joined), bufs)
     sources = beside(middle)
     over = over_segments(tails_near, [(3, 2)])
     chosen = call(choose_kernel, shape_of(2, 32, C), [VMEM] * 2)(tail, over)
     wrapped = over_segments(chosen, [(3, 0), (2, 1)])
-    out = pair_call(False, norm_gain, over, wrapped, sources, own, bufs)
+    out = pair_call(False, over, wrapped, sources, bufs)
     sent = lax.all_to_all(out, "shard", split_axis=0, concat_axis=0, tiled=True)
     main = jnp.concatenate([sent[:, 0:32], sent[:, 32:64]], axis=-1)
     decoded = main.reshape(32, 16, C).transpose(1, 0, 2)[None, None]

time: 155 us -> 166 us (1.071)
  the two profiles are of different devices: /device:TPU:2 before, /device:TPU:14 now
where the time goes in v2:
time: 166 us
  blocking collectives  61.9 us (37%)
  waiting for transfers between devices  48.8 us (29%)
  starting transfers between devices  33.2 us (20%)
  Pallas kernels  18 us (11%)
  local copies, waits for them, and re-layouts  2.83 us (2%)
    ppermute x8, waiting for transfers between devices, over_segments(): return lax.ppermute(array, 'segment', pairs)  43.4 us
    all_to_all x1, blocking collectives, body(): lax.all_to_all(chunks, 'shard', split_axis=0, concat_axis=0, tiled=True)  35.2 us
    all_to_all x1, blocking collectives, body(): sent = lax.all_to_all(out, 'shard', split_axis=0, concat_axis=0, tiled=True)  26.7 us
    ppermute x8, starting transfers between devices, over_segments(): return lax.ppermute(array, 'segment', pairs)  19.1 us
    pallas_call x2, Pallas kernels, pair_call(): call(functools.partial(pair_kernel, first), outs, [VMEM] * 5 + [HBM] * 2,...  13 us
    ppermute x2, starting transfers between devices, beside(): came_left = lax.ppermute(array, 'shard', up)  9.6 us
    ppermute x2, waiting for transfers between devices, beside(): came_right = lax.ppermute(array, 'shard', down)  4.22 us
  transfers between devices with their start and end apart: 13, of which 7 were waited for; matrix products, arithmetic and copies ran while one was open for 0% of the time, Pallas kernels for 0%

profile of v2, /device:TPU:14, one launch (start us, length us, event | category | flops | bytes accessed | tf_op | source)
XLA Modules:
  0.0 165.7 jit_solution(7816913868438838528)
XLA Ops:
  0.6 0.0 copy-start
  0.6 0.0 copy-start.2
  0.7 2.9 %shard_map.71.refs_0_ = bf16[1552,256]{1,0:T(8,128)(2,1)} custom-call(f32[1,256]{1,0:T(1,128)} %gain.1, bf16[1,3,256,256]{3,2,1,0:T(8,128)(2,1)} %taps_time.1, bf16[1,9,256,256]{3,2,1,0:T(8,128)(2,1)} %taps_space.1), custom_call_target="tpu_custom_call" | custom-call | flops 1048576 | bytes 1048576 | tf_op jit(solution)/shard_map/pallas_call | solution.py:336
  3.6 3.5 %collective-permute-start.7 = (bf16[1552,256]{1,0:T(8,128)(2,1)}, bf16[1552,256]{1,0:T(8,128)(2,1)S(1)}, u32[]{:S(2)}, u32[]{:S(2)}) collective-permute-start(bf16[1552,256]{1,0:T(8,128)(2,1)} %shard_map.71.refs_0_), channel_id=1, source_target_pairs={{0,128},{128,256},{256,384},{384,0},{1,129},{129,257},{257,385},{3... | collective-permute-start | bytes 2383880 | tf_op jit(solution)/shard_map/ppermute | solution.py:324
  7.1 2.8 %collective-permute-start.6 = (bf16[1552,256]{1,0:T(8,128)(2,1)}, bf16[1552,256]{1,0:T(8,128)(2,1)S(1)}, u32[]{:S(2)}, u32[]{:S(2)}) collective-permute-start(bf16[1552,256]{1,0:T(8,128)(2,1)} %shard_map.71.refs_0_), channel_id=1, source_target_pairs={{0,256},{128,384},{256,0},{384,128},{1,257},{129,385},{257,1},{385... | collective-permute-start | bytes 2383880 | tf_op jit(solution)/shard_map/ppermute | solution.py:324
  9.9 4.3 %collective-permute-start.5 = (bf16[1552,256]{1,0:T(8,128)(2,1)}, bf16[1552,256]{1,0:T(8,128)(2,1)S(1)}, u32[]{:S(2)}, u32[]{:S(2)}) collective-permute-start(bf16[1552,256]{1,0:T(8,128)(2,1)} %shard_map.71.refs_0_), channel_id=1, source_target_pairs={{0,384},{128,0},{256,128},{384,256},{1,385},{129,1},{257,129},{385... | collective-permute-start | bytes 2383880 | tf_op jit(solution)/shard_map/ppermute | solution.py:324
  14.3 12.0 %collective-permute-done.7.refs_3_ = bf16[1552,256]{1,0:T(8,128)(2,1)S(1)} collective-permute-done((bf16[1552,256]{1,0:T(8,128)(2,1)}, bf16[1552,256]{1,0:T(8,128)(2,1)S(1)}, u32[]{:S(2)}, u32[]{:S(2)}) %collective-permute-start.7) | collective-permute-done | bytes 794656 | tf_op jit(solution)/shard_map/ppermute | solution.py:324
  26.3 5.0 %collective-permute-done.6.refs_2_ = bf16[1552,256]{1,0:T(8,128)(2,1)S(1)} collective-permute-done((bf16[1552,256]{1,0:T(8,128)(2,1)}, bf16[1552,256]{1,0:T(8,128)(2,1)S(1)}, u32[]{:S(2)}, u32[]{:S(2)}) %collective-permute-start.6) | collective-permute-done | bytes 794656 | tf_op jit(solution)/shard_map/ppermute | solution.py:324
  31.3 15.6 %collective-permute-done.5.refs_1_ = bf16[1552,256]{1,0:T(8,128)(2,1)S(1)} collective-permute-done((bf16[1552,256]{1,0:T(8,128)(2,1)}, bf16[1552,256]{1,0:T(8,128)(2,1)S(1)}, u32[]{:S(2)}, u32[]{:S(2)}) %collective-permute-start.5) | collective-permute-done | bytes 794656 | tf_op jit(solution)/shard_map/ppermute | solution.py:324
  46.9 0.0 copy-start.1
  46.9 1.1 copy-done.1
  48.0 1.9 %shard_map.72.stacked = bf16[6208,256]{1,0:T(8,128)(2,1)} custom-call(bf16[1552,256]{1,0:T(8,128)(2,1)S(1)} %copy-done.1, bf16[1552,256]{1,0:T(8,128)(2,1)S(1)} %collective-permute-done.5.refs_1_, bf16[1552,256]{1,0:T(8,128)(2,1)S(1)} %collective-permute-done.6.refs_2_, bf16[1552,256]{1,0:T(8,128)(2,1)S(1)} %collective-permute-done.7.refs_3_), custom_call_target="tpu_custom_call" | custom-call | flops 1048576 | bytes 1048576 | tf_op jit(solution)/shard_map/pallas_call | solution.py:346
  50.0 1.9 %collective-permute-start.8 = (bf16[6208,256]{1,0:T(8,128)(2,1)}, bf16[6208,256]{1,0:T(8,128)(2,1)}, u32[]{:S(2)}, u32[]{:S(2)}) collective-permute-start(bf16[6208,256]{1,0:T(8,128)(2,1)} %shard_map.72.stacked), channel_id=1, source_target_pairs={{0,1},{1,0},{2,3},{3,2},{4,5},{5,4},{6,7},{7,6},{8,9},{9,8},{10,11... | collective-permute-start | bytes 9535496 | tf_op jit(solution)/shard_map/ppermute | solution.py:352
  51.9 0.0 copy-done
  52.0 0.2 copy.13
  52.1 0.0 copy-done.2
  52.1 0.1 shard_map.68
  52.2 35.2 %all_to_all.10.got = bf16[16,72,128]{2,1,0:T(8,128)(2,1)S(1)} all-to-all(bf16[16,72,128]{2,1,0:T(8,128)(2,1)S(1)} %shard_map.68), channel_id=1, replica_groups=mesh['segment'=4,'shard'=16,'stream'=8] {'shard'}, dimensions={0} | all-to-all | bytes 589824 | tf_op jit(solution)/shard_map/all_to_all | solution.py:334
  87.4 0.1 shard_map.69
  87.5 2.5 %collective-permute-start = (bf16[8,32,256]{2,1,0:T(8,128)(2,1)S(1)}, bf16[8,32,256]{2,1,0:T(8,128)(2,1)S(1)}, u32[]{:S(2)}, u32[]{:S(2)}) collective-permute-start(bf16[8,32,256]{2,1,0:T(8,128)(2,1)S(1)} %get-tuple-element.11), channel_id=1, source_target_pairs={{0,128},{128,256},{256,384},{1,129},{129,257},{257,385},{2,130},{1... | collective-permute-start | bytes 393224 | tf_op jit(solution)/shard_map/ppermute | solution.py:324
  90.0 3.3 %collective-permute-start.1 = (bf16[2,32,256]{2,1,0:T(8,128)(2,1)S(1)}, bf16[2,32,256]{2,1,0:T(8,128)(2,1)S(1)}, u32[]{:S(2)}, u32[]{:S(2)}) collective-permute-start(bf16[2,32,256]{2,1,0:T(8,128)(2,1)S(1)} %get-tuple-element.12.carry.wrapped), channel_id=1, source_target_pairs={{128,0},{384,256},{129,1},{385,257},{130,2},{386,258},{131,3},{387... | collective-permute-start | bytes 98312 | tf_op jit(solution)/shard_map/ppermute | solution.py:324
  93.4 1.6 collective-permute-done.1.near
  94.9 0.0 collective-permute-done.before
  95.0 1.3 collective-permute-start.4
  96.3 4.6 %collective-permute-start.3 = (bf16[24,32,256]{2,1,0:T(8,128)(2,1)S(1)}, bf16[24,32,256]{2,1,0:T(8,128)(2,1)S(1)}, u32[]{:S(2)}, u32[]{:S(2)}) collective-permute-start(bf16[24,32,256]{2,1,0:T(8,128)(2,1)S(1)} %get-tuple-element.14.mid), channel_id=1, source_target_pairs={{0,8},{8,16},{16,24},{24,32},{32,40},{40,48},{48,56},{56,64},{64,7... | collective-permute-start | bytes 1179656 | tf_op jit(solution)/shard_map/ppermute | solution.py:365
  100.9 0.7 collective-permute-start.2
  101.5 0.0 collective-permute-done.2.far
  101.5 4.2 %collective-permute-done.4.right = bf16[24,32,256]{2,1,0:T(8,128)(2,1)S(1)} collective-permute-done((bf16[24,32,256]{2,1,0:T(8,128)(2,1)S(1)}, bf16[24,32,256]{2,1,0:T(8,128)(2,1)S(1)}, u32[]{:S(2)}, u32[]{:S(2)}) %collective-permute-start.4) | collective-permute-done | bytes 393248 | tf_op jit(solution)/shard_map/ppermute | solution.py:366
  105.8 1.2 collective-permute-done.3.left
  106.9 0.0 collective-permute-done.8.swapped
  106.9 7.0 %shard_map.73 = (bf16[20,32,256]{2,1,0:T(8,128)(2,1)S(1)}, bf16[2,32,256]{2,1,0:T(8,128)(2,1)S(1)}, bf16[4,32,256]{2,1,0:T(8,128)(2,1)S(1)}) custom-call(bf16[4,32,256]{2,1,0:T(8,128)(2,1)S(1)} %collective-permute-done.2.far, bf16[2,32,256]{2,1,0:T(8,128)(2,1)S(1)} %get-tuple-element.12.carry.wrapped, bf16[24,32,256]{2,1,0:T(8,128)(2,1)S(1)} %get-tuple-element.14.mid, ...), custom_call_target="tpu_custom_call" | custom-call | flops 2147483648 | bytes 4194304 | tf_op jit(solution)/shard_map/pallas_call | solution.py:280
  113.9 1.3 collective-permute-start.12
  115.2 5.0 %collective-permute-start.11 = (bf16[20,32,256]{2,1,0:T(8,128)(2,1)S(1)}, bf16[20,32,256]{2,1,0:T(8,128)(2,1)S(1)}, u32[]{:S(2)}, u32[]{:S(2)}) collective-permute-start(bf16[20,32,256]{2,1,0:T(8,128)(2,1)S(1)} %get-tuple-element.17.mid), channel_id=1, source_target_pairs={{0,8},{8,16},{16,24},{24,32},{32,40},{40,48},{48,56},{56,64},{64,7... | collective-permute-start | bytes 983048 | tf_op jit(solution)/shard_map/ppermute | solution.py:365
  120.2 0.7 collective-permute-start.9
  120.9 0.0 collective-permute-done.9.came.far
  121.0 1.3 collective-permute-start.10
  122.3 9.1 %collective-permute-done.10.wrapped = bf16[2,32,256]{2,1,0:T(8,128)(2,1)S(1)} collective-permute-done((bf16[2,32,256]{2,1,0:T(8,128)(2,1)S(1)}, bf16[2,32,256]{2,1,0:T(8,128)(2,1)S(1)}, u32[]{:S(2)}, u32[]{:S(2)}) %collective-permute-start.10) | collective-permute-done | bytes 32800 | tf_op jit(solution)/shard_map/ppermute | solution.py:324
  131.4 0.0 collective-permute-done.12.right
  131.4 0.0 collective-permute-done.11.left
  131.4 6.0 %shard_map.75 = bf16[16,72,128]{2,1,0:T(8,128)(2,1)S(1)} custom-call(bf16[4,32,256]{2,1,0:T(8,128)(2,1)S(1)} %collective-permute-done.9.came.far, bf16[2,32,256]{2,1,0:T(8,128)(2,1)S(1)} %collective-permute-done.10.wrapped, bf16[20,32,256]{2,1,0:T(8,128)(2,1)S(1)} %get-tuple-element.17.mid, bf16[20,32,256]{2,1,0:T(8,128)(2,1)S(1)} %collective-permute-done.11.left, ...), custom_call_target="tpu_custom_call" | custom-call | flops 2147483648 | bytes 4194304 | tf_op jit(solution)/shard_map/pallas_call | solution.py:280
  137.4 26.7 %all_to_all.11 = bf16[16,72,128]{2,1,0:T(8,128)(2,1)S(1)} all-to-all(bf16[16,72,128]{2,1,0:T(8,128)(2,1)S(1)} %shard_map.75), channel_id=1, replica_groups=mesh['segment'=4,'shard'=16,'stream'=8] {'shard'}, dimensions={0} | all-to-all | bytes 589824 | tf_op jit(solution)/shard_map/all_to_all | solution.py:375
  164.2 0.8 copy.12
  165.1 0.6 reshape.16
  (9 shorter events, 0.2 us)
Async XLA Ops:
  0.6 51.3 %copy-start = (bf16[4,1,16,32,256]{4,3,2,1,0:T(8,128)(2,1)S(1)}, bf16[4,1,16,32,256]{4,3,2,1,0:T(8,128)(2,1)}, u32[]{:S(2)}) copy-start(bf16[4,1,16,32,256]{4,3,2,1,0:T(8,128)(2,1)} %param.5) | copy-start | bytes 3145732
  0.6 51.5 %copy-start.2 = (bf16[1,2,1,32,256]{4,3,2,1,0:T(8,128)(2,1)S(1)}, bf16[1,2,1,32,256]{4,3,2,1,0:T(8,128)(2,1)}, u32[]{:S(2)}) copy-start(bf16[1,2,1,32,256]{4,3,2,1,0:T(8,128)(2,1)} %param.9) | copy-start | bytes 98308
  3.6 22.7 %collective-permute-start.7 = (bf16[1552,256]{1,0:T(8,128)(2,1)}, bf16[1552,256]{1,0:T(8,128)(2,1)S(1)}, u32[]{:S(2)}, u32[]{:S(2)}) collective-permute-start(bf16[1552,256]{1,0:T(8,128)(2,1)} %shard_map.71.refs_0_), channel_id=1, source_target_pairs={{0,128},{128,256},{256,384},{384,0},{1,129},{129,257},{257,385},{3... | collective-permute-start | bytes 2383880 | tf_op jit(solution)/shard_map/ppermute | solution.py:324
  7.1 24.2 %collective-permute-start.6 = (bf16[1552,256]{1,0:T(8,128)(2,1)}, bf16[1552,256]{1,0:T(8,128)(2,1)S(1)}, u32[]{:S(2)}, u32[]{:S(2)}) collective-permute-start(bf16[1552,256]{1,0:T(8,128)(2,1)} %shard_map.71.refs_0_), channel_id=1, source_target_pairs={{0,256},{128,384},{256,0},{384,128},{1,257},{129,385},{257,1},{385... | collective-permute-start | bytes 2383880 | tf_op jit(solution)/shard_map/ppermute | solution.py:324
  9.9 37.0 %collective-permute-start.5 = (bf16[1552,256]{1,0:T(8,128)(2,1)}, bf16[1552,256]{1,0:T(8,128)(2,1)S(1)}, u32[]{:S(2)}, u32[]{:S(2)}) collective-permute-start(bf16[1552,256]{1,0:T(8,128)(2,1)} %shard_map.71.refs_0_), channel_id=1, source_target_pairs={{0,384},{128,0},{256,128},{384,256},{1,385},{129,1},{257,129},{385... | collective-permute-start | bytes 2383880 | tf_op jit(solution)/shard_map/ppermute | solution.py:324
  46.9 1.1 copy-start.1
  50.0 57.0 %collective-permute-start.8 = (bf16[6208,256]{1,0:T(8,128)(2,1)}, bf16[6208,256]{1,0:T(8,128)(2,1)}, u32[]{:S(2)}, u32[]{:S(2)}) collective-permute-start(bf16[6208,256]{1,0:T(8,128)(2,1)} %shard_map.72.stacked), channel_id=1, source_target_pairs={{0,1},{1,0},{2,3},{3,2},{4,5},{5,4},{6,7},{7,6},{8,9},{9,8},{10,11... | collective-permute-start | bytes 9535496 | tf_op jit(solution)/shard_map/ppermute | solution.py:352
  87.5 7.4 %collective-permute-start = (bf16[8,32,256]{2,1,0:T(8,128)(2,1)S(1)}, bf16[8,32,256]{2,1,0:T(8,128)(2,1)S(1)}, u32[]{:S(2)}, u32[]{:S(2)}) collective-permute-start(bf16[8,32,256]{2,1,0:T(8,128)(2,1)S(1)} %get-tuple-element.11), channel_id=1, source_target_pairs={{0,128},{128,256},{256,384},{1,129},{129,257},{257,385},{2,130},{1... | collective-permute-start | bytes 393224 | tf_op jit(solution)/shard_map/ppermute | solution.py:324
  90.0 4.9 %collective-permute-start.1 = (bf16[2,32,256]{2,1,0:T(8,128)(2,1)S(1)}, bf16[2,32,256]{2,1,0:T(8,128)(2,1)S(1)}, u32[]{:S(2)}, u32[]{:S(2)}) collective-permute-start(bf16[2,32,256]{2,1,0:T(8,128)(2,1)S(1)} %get-tuple-element.12.carry.wrapped), channel_id=1, source_target_pairs={{128,0},{384,256},{129,1},{385,257},{130,2},{386,258},{131,3},{387... | collective-permute-start | bytes 98312 | tf_op jit(solution)/shard_map/ppermute | solution.py:324
  95.0 10.8 %collective-permute-start.4 = (bf16[24,32,256]{2,1,0:T(8,128)(2,1)S(1)}, bf16[24,32,256]{2,1,0:T(8,128)(2,1)S(1)}, u32[]{:S(2)}, u32[]{:S(2)}) collective-permute-start(bf16[24,32,256]{2,1,0:T(8,128)(2,1)S(1)} %get-tuple-element.14.mid), channel_id=1, source_target_pairs={{8,0},{16,8},{24,16},{32,24},{40,32},{48,40},{56,48},{64,56},{72,6... | collective-permute-start | bytes 1179656 | tf_op jit(solution)/shard_map/ppermute | solution.py:366
  96.3 10.7 %collective-permute-start.3 = (bf16[24,32,256]{2,1,0:T(8,128)(2,1)S(1)}, bf16[24,32,256]{2,1,0:T(8,128)(2,1)S(1)}, u32[]{:S(2)}, u32[]{:S(2)}) collective-permute-start(bf16[24,32,256]{2,1,0:T(8,128)(2,1)S(1)} %get-tuple-element.14.mid), channel_id=1, source_target_pairs={{0,8},{8,16},{16,24},{24,32},{32,40},{40,48},{48,56},{56,64},{64,7... | collective-permute-start | bytes 1179656 | tf_op jit(solution)/shard_map/ppermute | solution.py:365
  100.9 0.7 collective-permute-start.2
  113.9 17.5 %collective-permute-start.12 = (bf16[20,32,256]{2,1,0:T(8,128)(2,1)S(1)}, bf16[20,32,256]{2,1,0:T(8,128)(2,1)S(1)}, u32[]{:S(2)}, u32[]{:S(2)}) collective-permute-start(bf16[20,32,256]{2,1,0:T(8,128)(2,1)S(1)} %get-tuple-element.17.mid), channel_id=1, source_target_pairs={{8,0},{16,8},{24,16},{32,24},{40,32},{48,40},{56,48},{64,56},{72,6... | collective-permute-start | bytes 983048 | tf_op jit(solution)/shard_map/ppermute | solution.py:366
  115.2 16.2 %collective-permute-start.11 = (bf16[20,32,256]{2,1,0:T(8,128)(2,1)S(1)}, bf16[20,32,256]{2,1,0:T(8,128)(2,1)S(1)}, u32[]{:S(2)}, u32[]{:S(2)}) collective-permute-start(bf16[20,32,256]{2,1,0:T(8,128)(2,1)S(1)} %get-tuple-element.17.mid), channel_id=1, source_target_pairs={{0,8},{8,16},{16,24},{24,32},{32,40},{40,48},{48,56},{56,64},{64,7... | collective-permute-start | bytes 983048 | tf_op jit(solution)/shard_map/ppermute | solution.py:365
  120.2 0.7 collective-permute-start.9
  121.0 10.4 %collective-permute-start.10 = (bf16[2,32,256]{2,1,0:T(8,128)(2,1)S(1)}, bf16[2,32,256]{2,1,0:T(8,128)(2,1)S(1)}, u32[]{:S(2)}, u32[]{:S(2)}) collective-permute-start(bf16[2,32,256]{2,1,0:T(8,128)(2,1)S(1)} %shard_map.74), channel_id=1, source_target_pairs={{384,0},{256,128},{385,1},{257,129},{386,2},{258,130},{387,3},{259... | collective-permute-start | bytes 98312 | tf_op jit(solution)/shard_map/ppermute | solution.py:324

commit v3 on v2

--- a/solution.py
+++ b/solution.py
@@ -175,11 +175,11 @@
     return slice(col * 16, col * 16 + 16)
 
 
-def pair_kernel(first, far, wrapped, mid, left, right, stacked, swapped, *rest):
+def pair_kernel(first, far, mid, left, right, stacked, swapped, *rest):
     if first:
         out, tails, tails_near = rest[:3]
     else:
-        (out,) = rest[:1]
+        out, tail_out = rest[:2]
     weights, terms, sems, gain_sem, normed, hidden, second, normed2 = rest[-8:]
     bufs = (stacked, swapped)
     section = 0 if first else 2
@@ -262,25 +262,30 @@
             out[0:4] = far[...]
 
     else:
-        carry = jnp.where(mine == 2, far[2:4], wrapped[...])
-        carry = jnp.where(mine == SECTIONS - 1, own_tail, carry)
-        for side in range(2):
-            lanes = slice(side * LANES, (side + 1) * LANES)
-            for n in range(4):
-                out[:, 64 + 4 * side + n, :] = carry[n // 2, cols(n % 2), lanes]
-
-
-def pair_call(first, far, wrapped, sources, bufs):
+        tail_out[...] = own_tail
+
+
+def place_kernel(_, own, came, wrapped, out):
+    mine = lax.axis_index("segment")
+    carry = jnp.where(mine == 2, came[2:4], wrapped[...])
+    carry = jnp.where(mine == SECTIONS - 1, own[...], carry)
+    for side in range(2):
+        lanes = slice(side * LANES, (side + 1) * LANES)
+        for n in range(4):
+            out[:, 4 * side + n, :] = carry[n // 2, cols(n % 2), lanes]
+
+
+def pair_call(first, far, sources, bufs):
     total = 24 if first else 20
     count = total - 2
     if first:
         outs = (shape_of(20, 32, C), shape_of(2, 32, C), shape_of(4, 32, C))
     else:
-        outs = shape_of(16, 72, LANES)
+        outs = (shape_of(16, 72, LANES), shape_of(2, 32, C))
     return call(
         functools.partial(pair_kernel, first),
         outs,
-        [VMEM] * 5 + [HBM] * 2,
+        [VMEM] * 4 + [HBM] * 2,
         [
             pltpu.VMEM((2, 2, GAIN_ROW, C), BF16),
             pltpu.VMEM((3, 16, C), BF16),
@@ -293,7 +298,25 @@
         ],
         flops=1 << 31,
         moved=4 << 20,
-    )(far, wrapped, *sources, *bufs)
+    )(far, *sources, *bufs)
+
+
+def place_call(out, own_tail, came, wrapped):
+    rows = pl.BlockSpec((16, 8, LANES), lambda i: (0, 8, 0))
+
+    def whole(array):
+        return pl.BlockSpec(array.shape, lambda i: (0,) * array.ndim)
+
+    return pl.pallas_call(
+        place_kernel,
+        out_shape=shape_of(16, 72, LANES),
+        grid=(1,),
+        in_specs=[pl.BlockSpec(memory_space=pl.ANY), whole(own_tail), whole(came), whole(wrapped)],
+        out_specs=rows,
+        input_output_aliases={0: 0},
+        name="place",
+        compiler_params=pltpu.CompilerParams(vmem_limit_bytes=16 << 20),
+    )(out, own_tail, came, wrapped)
 
 
 def join_kernel(frames, before, near, carry, out, both):
@@ -366,12 +389,13 @@
         came_right = lax.ppermute(array, "shard", down)
         return array, came_left, came_right
 
-    middle, tail, tails_near = pair_call(True, far, carry, beside(joined), bufs)
+    middle, tail, tails_near = pair_call(True, far, beside(joined), bufs)
     sources = beside(middle)
     over = over_segments(tails_near, [(3, 2)])
     chosen = call(choose_kernel, shape_of(2, 32, C), [VMEM] * 2)(tail, over)
     wrapped = over_segments(chosen, [(3, 0), (2, 1)])
-    out = pair_call(False, over, wrapped, sources, bufs)
+    out, own_tail = pair_call(False, over, sources, bufs)
+    out = place_call(out, own_tail, over, wrapped)
     sent = lax.all_to_all(out, "shard", split_axis=0, concat_axis=0, tiled=True)
     main = jnp.concatenate([sent[:, 0:32], sent[:, 32:64]], axis=-1)
     decoded = main.reshape(32, 16, C).transpose(1, 0, 2)[None, None]

time: 166 us -> 164 us (0.988)
  the two profiles are of different devices: /device:TPU:14 before, /device:TPU:48 now
where the time goes in v3:
time: 164 us; the launch traced here: 163 us
  blocking collectives  62 us (38%)
  waiting for transfers between devices  46.4 us (28%)
  starting transfers between devices  32.9 us (20%)
  Pallas kernels  18.1 us (11%)
  local copies, waits for them, and re-layouts  2.83 us (2%)
    ppermute x8, waiting for transfers between devices, over_segments(): return lax.ppermute(array, 'segment', pairs)  44.9 us
    all_to_all x1, blocking collectives, body(): lax.all_to_all(chunks, 'shard', split_axis=0, concat_axis=0, tiled=True)  34.6 us
    all_to_all x1, blocking collectives, body(): sent = lax.all_to_all(out, 'shard', split_axis=0, concat_axis=0, tiled=True)  27.5 us
    ppermute x8, starting transfers between devices, over_segments(): return lax.ppermute(array, 'segment', pairs)  19.3 us
    pallas_call x2, Pallas kernels, pair_call(): call(functools.partial(pair_kernel, first), outs, [VMEM] * 4 + [HBM] * 2,...  12.9 us
    ppermute x2, starting transfers between devices, beside(): came_left = lax.ppermute(array, 'shard', up)  7.09 us
    ppermute x2, starting transfers between devices, beside(): came_right = lax.ppermute(array, 'shard', down)  4.6 us
  transfers between devices with their start and end apart: 13, of which 6 were waited for; matrix products, arithmetic and copies ran while one was open for 0% of the time, Pallas kernels for 4%

profile of v3, /device:TPU:48, one launch (start us, length us, event | category | flops | bytes accessed | tf_op | source)
XLA Modules:
  0.0 163.2 jit_solution(11535948544393435304)
XLA Ops:
  0.6 0.0 copy-start
  0.6 0.0 copy-start.2
  0.7 2.9 %shard_map.71.refs_0_ = bf16[1552,256]{1,0:T(8,128)(2,1)} custom-call(f32[1,256]{1,0:T(1,128)} %gain.1, bf16[1,3,256,256]{3,2,1,0:T(8,128)(2,1)} %taps_time.1, bf16[1,9,256,256]{3,2,1,0:T(8,128)(2,1)} %taps_space.1), custom_call_target="tpu_custom_call" | custom-call | flops 1048576 | bytes 1048576 | tf_op jit(solution)/shard_map/pallas_call | solution.py:359
  3.6 3.2 %collective-permute-start.7 = (bf16[1552,256]{1,0:T(8,128)(2,1)}, bf16[1552,256]{1,0:T(8,128)(2,1)S(1)}, u32[]{:S(2)}, u32[]{:S(2)}) collective-permute-start(bf16[1552,256]{1,0:T(8,128)(2,1)} %shard_map.71.refs_0_), channel_id=1, source_target_pairs={{0,128},{128,256},{256,384},{384,0},{1,129},{129,257},{257,385},{3... | collective-permute-start | bytes 2383880 | tf_op jit(solution)/shard_map/ppermute | solution.py:347
  6.8 2.5 %collective-permute-start.6 = (bf16[1552,256]{1,0:T(8,128)(2,1)}, bf16[1552,256]{1,0:T(8,128)(2,1)S(1)}, u32[]{:S(2)}, u32[]{:S(2)}) collective-permute-start(bf16[1552,256]{1,0:T(8,128)(2,1)} %shard_map.71.refs_0_), channel_id=1, source_target_pairs={{0,256},{128,384},{256,0},{384,128},{1,257},{129,385},{257,1},{385... | collective-permute-start | bytes 2383880 | tf_op jit(solution)/shard_map/ppermute | solution.py:347
  9.3 3.0 %collective-permute-start.5 = (bf16[1552,256]{1,0:T(8,128)(2,1)}, bf16[1552,256]{1,0:T(8,128)(2,1)S(1)}, u32[]{:S(2)}, u32[]{:S(2)}) collective-permute-start(bf16[1552,256]{1,0:T(8,128)(2,1)} %shard_map.71.refs_0_), channel_id=1, source_target_pairs={{0,384},{128,0},{256,128},{384,256},{1,385},{129,1},{257,129},{385... | collective-permute-start | bytes 2383880 | tf_op jit(solution)/shard_map/ppermute | solution.py:347
  12.3 29.9 %collective-permute-done.7.refs_3_ = bf16[1552,256]{1,0:T(8,128)(2,1)S(1)} collective-permute-done((bf16[1552,256]{1,0:T(8,128)(2,1)}, bf16[1552,256]{1,0:T(8,128)(2,1)S(1)}, u32[]{:S(2)}, u32[]{:S(2)}) %collective-permute-start.7) | collective-permute-done | bytes 794656 | tf_op jit(solution)/shard_map/ppermute | solution.py:347
  42.2 0.0 collective-permute-done.6.refs_2_
  42.2 3.7 %collective-permute-done.5.refs_1_ = bf16[1552,256]{1,0:T(8,128)(2,1)S(1)} collective-permute-done((bf16[1552,256]{1,0:T(8,128)(2,1)}, bf16[1552,256]{1,0:T(8,128)(2,1)S(1)}, u32[]{:S(2)}, u32[]{:S(2)}) %collective-permute-start.5) | collective-permute-done | bytes 794656 | tf_op jit(solution)/shard_map/ppermute | solution.py:347
  45.9 0.0 copy-start.1
  45.9 1.1 copy-done.1
  47.1 1.9 %shard_map.72.stacked = bf16[6208,256]{1,0:T(8,128)(2,1)} custom-call(bf16[1552,256]{1,0:T(8,128)(2,1)S(1)} %copy-done.1, bf16[1552,256]{1,0:T(8,128)(2,1)S(1)} %collective-permute-done.5.refs_1_, bf16[1552,256]{1,0:T(8,128)(2,1)S(1)} %collective-permute-done.6.refs_2_, bf16[1552,256]{1,0:T(8,128)(2,1)S(1)} %collective-permute-done.7.refs_3_), custom_call_target="tpu_custom_call" | custom-call | flops 1048576 | bytes 1048576 | tf_op jit(solution)/shard_map/pallas_call | solution.py:369
  49.0 1.9 %collective-permute-start.8 = (bf16[6208,256]{1,0:T(8,128)(2,1)}, bf16[6208,256]{1,0:T(8,128)(2,1)}, u32[]{:S(2)}, u32[]{:S(2)}) collective-permute-start(bf16[6208,256]{1,0:T(8,128)(2,1)} %shard_map.72.stacked), channel_id=1, source_target_pairs={{0,1},{1,0},{2,3},{3,2},{4,5},{5,4},{6,7},{7,6},{8,9},{9,8},{10,11... | collective-permute-start | bytes 9535496 | tf_op jit(solution)/shard_map/ppermute | solution.py:375
  51.0 0.0 copy-done
  51.0 0.2 copy.14
  51.1 0.0 copy-done.2
  51.2 0.1 shard_map.68
  51.2 34.6 %all_to_all.10.got = bf16[16,72,128]{2,1,0:T(8,128)(2,1)S(1)} all-to-all(bf16[16,72,128]{2,1,0:T(8,128)(2,1)S(1)} %shard_map.68), channel_id=1, replica_groups=mesh['segment'=4,'shard'=16,'stream'=8] {'shard'}, dimensions={0} | all-to-all | bytes 589824 | tf_op jit(solution)/shard_map/all_to_all | solution.py:357
  85.8 0.1 shard_map.69
  85.9 2.9 %collective-permute-start = (bf16[8,32,256]{2,1,0:T(8,128)(2,1)S(1)}, bf16[8,32,256]{2,1,0:T(8,128)(2,1)S(1)}, u32[]{:S(2)}, u32[]{:S(2)}) collective-permute-start(bf16[8,32,256]{2,1,0:T(8,128)(2,1)S(1)} %get-tuple-element.13), channel_id=1, source_target_pairs={{0,128},{128,256},{256,384},{1,129},{129,257},{257,385},{2,130},{1... | collective-permute-start | bytes 393224 | tf_op jit(solution)/shard_map/ppermute | solution.py:347
  88.8 1.3 collective-permute-start.1
  90.1 4.5 %collective-permute-done.1.near = bf16[2,32,256]{2,1,0:T(8,128)(2,1)S(1)} collective-permute-done((bf16[2,32,256]{2,1,0:T(8,128)(2,1)S(1)}, bf16[2,32,256]{2,1,0:T(8,128)(2,1)S(1)}, u32[]{:S(2)}, u32[]{:S(2)}) %collective-permute-start.1) | collective-permute-done | bytes 32800 | tf_op jit(solution)/shard_map/ppermute | solution.py:347
  94.6 0.0 collective-permute-done.before
  94.6 2.7 %collective-permute-start.4 = (bf16[24,32,256]{2,1,0:T(8,128)(2,1)S(1)}, bf16[24,32,256]{2,1,0:T(8,128)(2,1)S(1)}, u32[]{:S(2)}, u32[]{:S(2)}) collective-permute-start(bf16[24,32,256]{2,1,0:T(8,128)(2,1)S(1)} %get-tuple-element.16.mid), channel_id=1, source_target_pairs={{8,0},{16,8},{24,16},{32,24},{40,32},{48,40},{56,48},{64,56},{72,6... | collective-permute-start | bytes 1179656 | tf_op jit(solution)/shard_map/ppermute | solution.py:389
  97.3 3.2 %collective-permute-start.3 = (bf16[24,32,256]{2,1,0:T(8,128)(2,1)S(1)}, bf16[24,32,256]{2,1,0:T(8,128)(2,1)S(1)}, u32[]{:S(2)}, u32[]{:S(2)}) collective-permute-start(bf16[24,32,256]{2,1,0:T(8,128)(2,1)S(1)} %get-tuple-element.16.mid), channel_id=1, source_target_pairs={{0,8},{8,16},{16,24},{24,32},{32,40},{40,48},{48,56},{56,64},{64,7... | collective-permute-start | bytes 1179656 | tf_op jit(solution)/shard_map/ppermute | solution.py:388
  100.5 3.8 %collective-permute-start.2 = (bf16[4,32,256]{2,1,0:T(8,128)(2,1)S(1)}, bf16[4,32,256]{2,1,0:T(8,128)(2,1)S(1)}, u32[]{:S(2)}, u32[]{:S(2)}) collective-permute-start(bf16[4,32,256]{2,1,0:T(8,128)(2,1)S(1)} %get-tuple-element.15), channel_id=1, source_target_pairs={{256,0},{257,1},{258,2},{259,3},{260,4},{261,5},{262,6},{263,7},{2... | collective-permute-start | bytes 196616 | tf_op jit(solution)/shard_map/ppermute | solution.py:347
  104.3 1.9 %collective-permute-done.2.far = bf16[4,32,256]{2,1,0:T(8,128)(2,1)S(1)} collective-permute-done((bf16[4,32,256]{2,1,0:T(8,128)(2,1)S(1)}, bf16[4,32,256]{2,1,0:T(8,128)(2,1)S(1)}, u32[]{:S(2)}, u32[]{:S(2)}) %collective-permute-start.2) | collective-permute-done | bytes 65568 | tf_op jit(solution)/shard_map/ppermute | solution.py:347
  106.2 0.0 collective-permute-done.4.right
  106.2 1.5 collective-permute-done.3.left
  107.7 0.0 collective-permute-done.8.swapped
  107.7 7.0 %shard_map.73 = (bf16[20,32,256]{2,1,0:T(8,128)(2,1)S(1)}, bf16[2,32,256]{2,1,0:T(8,128)(2,1)S(1)}, bf16[4,32,256]{2,1,0:T(8,128)(2,1)S(1)}) custom-call(bf16[4,32,256]{2,1,0:T(8,128)(2,1)S(1)} %collective-permute-done.2.far, bf16[24,32,256]{2,1,0:T(8,128)(2,1)S(1)} %get-tuple-element.16.mid, bf16[24,32,256]{2,1,0:T(8,128)(2,1)S(1)} %collective-permute-done.3.left, ...), custom_call_target="tpu_custom_call" | custom-call | flops 2147483648 | bytes 4194304 | tf_op jit(solution)/shard_map/pallas_call | solution.py:285
  114.7 1.9 %collective-permute-start.11 = (bf16[20,32,256]{2,1,0:T(8,128)(2,1)S(1)}, bf16[20,32,256]{2,1,0:T(8,128)(2,1)S(1)}, u32[]{:S(2)}, u32[]{:S(2)}) collective-permute-start(bf16[20,32,256]{2,1,0:T(8,128)(2,1)S(1)} %get-tuple-element.18.mid), channel_id=1, source_target_pairs={{8,0},{16,8},{24,16},{32,24},{40,32},{48,40},{56,48},{64,56},{72,6... | collective-permute-start | bytes 983048 | tf_op jit(solution)/shard_map/ppermute | solution.py:389
  116.6 3.9 %collective-permute-start.10 = (bf16[20,32,256]{2,1,0:T(8,128)(2,1)S(1)}, bf16[20,32,256]{2,1,0:T(8,128)(2,1)S(1)}, u32[]{:S(2)}, u32[]{:S(2)}) collective-permute-start(bf16[20,32,256]{2,1,0:T(8,128)(2,1)S(1)} %get-tuple-element.18.mid), channel_id=1, source_target_pairs={{0,8},{8,16},{16,24},{24,32},{32,40},{40,48},{48,56},{56,64},{64,7... | collective-permute-start | bytes 983048 | tf_op jit(solution)/shard_map/ppermute | solution.py:388
  120.6 1.3 collective-permute-start.9
  121.9 4.9 %collective-permute-done.9.far.came = bf16[4,32,256]{2,1,0:T(8,128)(2,1)S(1)} collective-permute-done((bf16[4,32,256]{2,1,0:T(8,128)(2,1)S(1)}, bf16[4,32,256]{2,1,0:T(8,128)(2,1)S(1)}, u32[]{:S(2)}, u32[]{:S(2)}) %collective-permute-start.9) | collective-permute-done | bytes 65568 | tf_op jit(solution)/shard_map/ppermute | solution.py:347
  126.7 1.3 collective-permute-start.12
  128.0 0.0 collective-permute-done.11.right
  128.0 0.0 collective-permute-done.10.left
  128.1 6.0 %shard_map.74 = (bf16[16,72,128]{2,1,0:T(8,128)(2,1)S(1)}, bf16[2,32,256]{2,1,0:T(8,128)(2,1)S(1)}) custom-call(bf16[4,32,256]{2,1,0:T(8,128)(2,1)S(1)} %collective-permute-done.9.far.came, bf16[20,32,256]{2,1,0:T(8,128)(2,1)S(1)} %get-tuple-element.18.mid, bf16[20,32,256]{2,1,0:T(8,128)(2,1)S(1)} %collective-permute-done.10.left, ...), custom_call_target="tpu_custom_call" | custom-call | flops 2147483648 | bytes 4194304 | tf_op jit(solution)/shard_map/pallas_call | solution.py:285
  134.0 0.0 collective-permute-done.12.wrapped
  134.1 0.1 place.1
  134.2 27.5 %all_to_all.11 = bf16[16,72,128]{2,1,0:T(8,128)(2,1)S(1)} all-to-all(bf16[16,72,128]{2,1,0:T(8,128)(2,1)S(1)} %place.1), channel_id=1, replica_groups=mesh['segment'=4,'shard'=16,'stream'=8] {'shard'}, dimensions={0} | all-to-all | bytes 589824 | tf_op jit(solution)/shard_map/all_to_all | solution.py:399
  161.7 0.8 copy.13
  162.6 0.6 reshape.16
  (9 shorter events, 0.2 us)
Async XLA Ops:
  0.6 50.3 %copy-start = (bf16[4,1,16,32,256]{4,3,2,1,0:T(8,128)(2,1)S(1)}, bf16[4,1,16,32,256]{4,3,2,1,0:T(8,128)(2,1)}, u32[]{:S(2)}) copy-start(bf16[4,1,16,32,256]{4,3,2,1,0:T(8,128)(2,1)} %param.5) | copy-start | bytes 3145732
  0.6 50.5 %copy-start.2 = (bf16[1,2,1,32,256]{4,3,2,1,0:T(8,128)(2,1)S(1)}, bf16[1,2,1,32,256]{4,3,2,1,0:T(8,128)(2,1)}, u32[]{:S(2)}) copy-start(bf16[1,2,1,32,256]{4,3,2,1,0:T(8,128)(2,1)} %param.9) | copy-start | bytes 98308
  3.6 38.6 %collective-permute-start.7 = (bf16[1552,256]{1,0:T(8,128)(2,1)}, bf16[1552,256]{1,0:T(8,128)(2,1)S(1)}, u32[]{:S(2)}, u32[]{:S(2)}) collective-permute-start(bf16[1552,256]{1,0:T(8,128)(2,1)} %shard_map.71.refs_0_), channel_id=1, source_target_pairs={{0,128},{128,256},{256,384},{384,0},{1,129},{129,257},{257,385},{3... | collective-permute-start | bytes 2383880 | tf_op jit(solution)/shard_map/ppermute | solution.py:347
  6.8 35.4 %collective-permute-start.6 = (bf16[1552,256]{1,0:T(8,128)(2,1)}, bf16[1552,256]{1,0:T(8,128)(2,1)S(1)}, u32[]{:S(2)}, u32[]{:S(2)}) collective-permute-start(bf16[1552,256]{1,0:T(8,128)(2,1)} %shard_map.71.refs_0_), channel_id=1, source_target_pairs={{0,256},{128,384},{256,0},{384,128},{1,257},{129,385},{257,1},{385... | collective-permute-start | bytes 2383880 | tf_op jit(solution)/shard_map/ppermute | solution.py:347
  9.3 36.6 %collective-permute-start.5 = (bf16[1552,256]{1,0:T(8,128)(2,1)}, bf16[1552,256]{1,0:T(8,128)(2,1)S(1)}, u32[]{:S(2)}, u32[]{:S(2)}) collective-permute-start(bf16[1552,256]{1,0:T(8,128)(2,1)} %shard_map.71.refs_0_), channel_id=1, source_target_pairs={{0,384},{128,0},{256,128},{384,256},{1,385},{129,1},{257,129},{385... | collective-permute-start | bytes 2383880 | tf_op jit(solution)/shard_map/ppermute | solution.py:347
  45.9 1.1 copy-start.1
  49.0 58.7 %collective-permute-start.8 = (bf16[6208,256]{1,0:T(8,128)(2,1)}, bf16[6208,256]{1,0:T(8,128)(2,1)}, u32[]{:S(2)}, u32[]{:S(2)}) collective-permute-start(bf16[6208,256]{1,0:T(8,128)(2,1)} %shard_map.72.stacked), channel_id=1, source_target_pairs={{0,1},{1,0},{2,3},{3,2},{4,5},{5,4},{6,7},{7,6},{8,9},{9,8},{10,11... | collective-permute-start | bytes 9535496 | tf_op jit(solution)/shard_map/ppermute | solution.py:375
  85.9 8.7 %collective-permute-start = (bf16[8,32,256]{2,1,0:T(8,128)(2,1)S(1)}, bf16[8,32,256]{2,1,0:T(8,128)(2,1)S(1)}, u32[]{:S(2)}, u32[]{:S(2)}) collective-permute-start(bf16[8,32,256]{2,1,0:T(8,128)(2,1)S(1)} %get-tuple-element.13), channel_id=1, source_target_pairs={{0,128},{128,256},{256,384},{1,129},{129,257},{257,385},{2,130},{1... | collective-permute-start | bytes 393224 | tf_op jit(solution)/shard_map/ppermute | solution.py:347
  88.8 5.8 %collective-permute-start.1 = (bf16[2,32,256]{2,1,0:T(8,128)(2,1)S(1)}, bf16[2,32,256]{2,1,0:T(8,128)(2,1)S(1)}, u32[]{:S(2)}, u32[]{:S(2)}) collective-permute-start(bf16[2,32,256]{2,1,0:T(8,128)(2,1)S(1)} %get-tuple-element.14.carry), channel_id=1, source_target_pairs={{128,0},{384,256},{129,1},{385,257},{130,2},{386,258},{131,3},{387... | collective-permute-start | bytes 98312 | tf_op jit(solution)/shard_map/ppermute | solution.py:347
  94.6 11.6 %collective-permute-start.4 = (bf16[24,32,256]{2,1,0:T(8,128)(2,1)S(1)}, bf16[24,32,256]{2,1,0:T(8,128)(2,1)S(1)}, u32[]{:S(2)}, u32[]{:S(2)}) collective-permute-start(bf16[24,32,256]{2,1,0:T(8,128)(2,1)S(1)} %get-tuple-element.16.mid), channel_id=1, source_target_pairs={{8,0},{16,8},{24,16},{32,24},{40,32},{48,40},{56,48},{64,56},{72,6... | collective-permute-start | bytes 1179656 | tf_op jit(solution)/shard_map/ppermute | solution.py:389
  97.3 10.4 %collective-permute-start.3 = (bf16[24,32,256]{2,1,0:T(8,128)(2,1)S(1)}, bf16[24,32,256]{2,1,0:T(8,128)(2,1)S(1)}, u32[]{:S(2)}, u32[]{:S(2)}) collective-permute-start(bf16[24,32,256]{2,1,0:T(8,128)(2,1)S(1)} %get-tuple-element.16.mid), channel_id=1, source_target_pairs={{0,8},{8,16},{16,24},{24,32},{32,40},{40,48},{48,56},{56,64},{64,7... | collective-permute-start | bytes 1179656 | tf_op jit(solution)/shard_map/ppermute | solution.py:388
  100.5 5.7 %collective-permute-start.2 = (bf16[4,32,256]{2,1,0:T(8,128)(2,1)S(1)}, bf16[4,32,256]{2,1,0:T(8,128)(2,1)S(1)}, u32[]{:S(2)}, u32[]{:S(2)}) collective-permute-start(bf16[4,32,256]{2,1,0:T(8,128)(2,1)S(1)} %get-tuple-element.15), channel_id=1, source_target_pairs={{256,0},{257,1},{258,2},{259,3},{260,4},{261,5},{262,6},{263,7},{2... | collective-permute-start | bytes 196616 | tf_op jit(solution)/shard_map/ppermute | solution.py:347
  114.7 13.3 %collective-permute-start.11 = (bf16[20,32,256]{2,1,0:T(8,128)(2,1)S(1)}, bf16[20,32,256]{2,1,0:T(8,128)(2,1)S(1)}, u32[]{:S(2)}, u32[]{:S(2)}) collective-permute-start(bf16[20,32,256]{2,1,0:T(8,128)(2,1)S(1)} %get-tuple-element.18.mid), channel_id=1, source_target_pairs={{8,0},{16,8},{24,16},{32,24},{40,32},{48,40},{56,48},{64,56},{72,6... | collective-permute-start | bytes 983048 | tf_op jit(solution)/shard_map/ppermute | solution.py:389
  116.6 11.4 %collective-permute-start.10 = (bf16[20,32,256]{2,1,0:T(8,128)(2,1)S(1)}, bf16[20,32,256]{2,1,0:T(8,128)(2,1)S(1)}, u32[]{:S(2)}, u32[]{:S(2)}) collective-permute-start(bf16[20,32,256]{2,1,0:T(8,128)(2,1)S(1)} %get-tuple-element.18.mid), channel_id=1, source_target_pairs={{0,8},{8,16},{16,24},{24,32},{32,40},{40,48},{48,56},{56,64},{64,7... | collective-permute-start | bytes 983048 | tf_op jit(solution)/shard_map/ppermute | solution.py:388
  120.6 6.2 %collective-permute-start.9 = (bf16[4,32,256]{2,1,0:T(8,128)(2,1)S(1)}, bf16[4,32,256]{2,1,0:T(8,128)(2,1)S(1)}, u32[]{:S(2)}, u32[]{:S(2)}) collective-permute-start(bf16[4,32,256]{2,1,0:T(8,128)(2,1)S(1)} %get-tuple-element.17), channel_id=1, source_target_pairs={{384,256},{385,257},{386,258},{387,259},{388,260},{389,261},{390,2... | collective-permute-start | bytes 196616 | tf_op jit(solution)/shard_map/ppermute | solution.py:347
  126.7 7.3 %collective-permute-start.12 = (bf16[2,32,256]{2,1,0:T(8,128)(2,1)S(1)}, bf16[2,32,256]{2,1,0:T(8,128)(2,1)S(1)}, u32[]{:S(2)}, u32[]{:S(2)}) collective-permute-start(bf16[2,32,256]{2,1,0:T(8,128)(2,1)S(1)} %shard_map.75), channel_id=1, source_target_pairs={{384,0},{256,128},{385,1},{257,129},{386,2},{258,130},{387,3},{259... | collective-permute-start | bytes 98312 | tf_op jit(solution)/shard_map/ppermute | solution.py:347

commit v4 on v3

--- a/solution.py
+++ b/solution.py
@@ -175,7 +175,7 @@
     return slice(col * 16, col * 16 + 16)
 
 
-def pair_kernel(first, far, mid, left, right, stacked, swapped, *rest):
+def pair_kernel(first, mid, left, right, stacked, swapped, *rest):
     if first:
         out, tails, tails_near = rest[:3]
     else:
@@ -256,11 +256,6 @@
         row = rows[0:1] + (rows[1:2] + rows[2:3])
         last = out[count - 2 : count].astype(F32).reshape(64, C)
         tails_near[2:4] = normed_of(last, row).reshape(2, 32, C)
-
-        @pl.when(mine == 0)
-        def _():
-            out[0:4] = far[...]
-
     else:
         tail_out[...] = own_tail
 
@@ -275,7 +270,7 @@
             out[:, 4 * side + n, :] = carry[n // 2, cols(n % 2), lanes]
 
 
-def pair_call(first, far, sources, bufs):
+def pair_call(first, sources, bufs):
     total = 24 if first else 20
     count = total - 2
     if first:
@@ -285,7 +280,7 @@
     return call(
         functools.partial(pair_kernel, first),
         outs,
-        [VMEM] * 4 + [HBM] * 2,
+        [VMEM] * 3 + [HBM] * 2,
         [
             pltpu.VMEM((2, 2, GAIN_ROW, C), BF16),
             pltpu.VMEM((3, 16, C), BF16),
@@ -298,7 +293,25 @@
         ],
         flops=1 << 31,
         moved=4 << 20,
-    )(far, *sources, *bufs)
+    )(*sources, *bufs)
+
+
+def later_kernel(frames, far, out):
+    out[...] = jnp.where(lax.axis_index("segment") == 0, far[...], frames[...])
+
+
+def later_call(middle, far):
+    rows = pl.BlockSpec((4, 32, C), lambda i: (0, 0, 0))
+    return pl.pallas_call(
+        later_kernel,
+        out_shape=shape_of(20, 32, C),
+        grid=(1,),
+        in_specs=[rows, rows],
+        out_specs=rows,
+        input_output_aliases={0: 0},
+        name="later",
+        compiler_params=pltpu.CompilerParams(vmem_limit_bytes=16 << 20),
+    )(middle, far)
 
 
 def place_call(out, own_tail, came, wrapped):
@@ -389,12 +402,13 @@
         came_right = lax.ppermute(array, "shard", down)
         return array, came_left, came_right
 
-    middle, tail, tails_near = pair_call(True, far, beside(joined), bufs)
+    middle, tail, tails_near = pair_call(True, beside(joined), bufs)
+    middle = later_call(middle, far)
     sources = beside(middle)
     over = over_segments(tails_near, [(3, 2)])
     chosen = call(choose_kernel, shape_of(2, 32, C), [VMEM] * 2)(tail, over)
     wrapped = over_segments(chosen, [(3, 0), (2, 1)])
-    out, own_tail = pair_call(False, over, sources, bufs)
+    out, own_tail = pair_call(False, sources, bufs)
     out = place_call(out, own_tail, over, wrapped)
     sent = lax.all_to_all(out, "shard", split_axis=0, concat_axis=0, tiled=True)
     main = jnp.concatenate([sent[:, 0:32], sent[:, 32:64]], axis=-1)

time: 164 us -> 164 us (level)
  the two profiles are of different devices: /device:TPU:48 before, /device:TPU:38 now
where the time goes in v4:
time: 164 us; the launch traced here: 163 us
  blocking collectives  63.3 us (39%)
  waiting for transfers between devices  44.1 us (27%)
  starting transfers between devices  34.1 us (21%)
  Pallas kernels  18.1 us (11%)
  local copies, waits for them, and re-layouts  2.83 us (2%)
    ppermute x8, waiting for transfers between devices, over_segments(): return lax.ppermute(array, 'segment', pairs)  35.4 us
    all_to_all x1, blocking collectives, body(): lax.all_to_all(chunks, 'shard', split_axis=0, concat_axis=0, tiled=True)  34.6 us
    all_to_all x1, blocking collectives, body(): sent = lax.all_to_all(out, 'shard', split_axis=0, concat_axis=0, tiled=True)  28.8 us
    ppermute x8, starting transfers between devices, over_segments(): return lax.ppermute(array, 'segment', pairs)  20.5 us
    pallas_call x2, Pallas kernels, pair_call(): call(functools.partial(pair_kernel, first), outs, [VMEM] * 3 + [HBM] * 2,...  12.9 us
    ppermute x2, starting transfers between devices, beside(): came_left = lax.ppermute(array, 'shard', up)  7.09 us
    ppermute x2, waiting for transfers between devices, beside(): came_right = lax.ppermute(array, 'shard', down)  4.91 us
    ppermute x2, starting transfers between devices, beside(): came_right = lax.ppermute(array, 'shard', down)  4.6 us
  transfers between devices with their start and end apart: 13, of which 8 were waited for; matrix products, arithmetic and copies ran while one was open for 0% of the time, Pallas kernels for 8%

profile of v4, /device:TPU:38, one launch (start us, length us, event | category | flops | bytes accessed | tf_op | source)
XLA Modules:
  0.0 163.5 jit_solution(10119816798953405097)
XLA Ops:
  0.6 0.0 copy-start
  0.6 0.0 copy-start.2
  0.7 2.9 %shard_map.71.refs_0_ = bf16[1552,256]{1,0:T(8,128)(2,1)} custom-call(f32[1,256]{1,0:T(1,128)} %gain.1, bf16[1,3,256,256]{3,2,1,0:T(8,128)(2,1)} %taps_time.1, bf16[1,9,256,256]{3,2,1,0:T(8,128)(2,1)} %taps_space.1), custom_call_target="tpu_custom_call" | custom-call | flops 1048576 | bytes 1048576 | tf_op jit(solution)/shard_map/pallas_call | solution.py:372
  3.6 3.5 %collective-permute-start.6 = (bf16[1552,256]{1,0:T(8,128)(2,1)}, bf16[1552,256]{1,0:T(8,128)(2,1)S(1)}, u32[]{:S(2)}, u32[]{:S(2)}) collective-permute-start(bf16[1552,256]{1,0:T(8,128)(2,1)} %shard_map.71.refs_0_), channel_id=1, source_target_pairs={{0,128},{128,256},{256,384},{384,0},{1,129},{129,257},{257,385},{3... | collective-permute-start | bytes 2383880 | tf_op jit(solution)/shard_map/ppermute | solution.py:360
  7.1 4.8 %collective-permute-start.5 = (bf16[1552,256]{1,0:T(8,128)(2,1)}, bf16[1552,256]{1,0:T(8,128)(2,1)S(1)}, u32[]{:S(2)}, u32[]{:S(2)}) collective-permute-start(bf16[1552,256]{1,0:T(8,128)(2,1)} %shard_map.71.refs_0_), channel_id=1, source_target_pairs={{0,256},{128,384},{256,0},{384,128},{1,257},{129,385},{257,1},{385... | collective-permute-start | bytes 2383880 | tf_op jit(solution)/shard_map/ppermute | solution.py:360
  11.9 3.3 %collective-permute-start.4 = (bf16[1552,256]{1,0:T(8,128)(2,1)}, bf16[1552,256]{1,0:T(8,128)(2,1)S(1)}, u32[]{:S(2)}, u32[]{:S(2)}) collective-permute-start(bf16[1552,256]{1,0:T(8,128)(2,1)} %shard_map.71.refs_0_), channel_id=1, source_target_pairs={{0,384},{128,0},{256,128},{384,256},{1,385},{129,1},{257,129},{385... | collective-permute-start | bytes 2383880 | tf_op jit(solution)/shard_map/ppermute | solution.py:360
  15.2 11.3 %collective-permute-done.6.refs_3_ = bf16[1552,256]{1,0:T(8,128)(2,1)S(1)} collective-permute-done((bf16[1552,256]{1,0:T(8,128)(2,1)}, bf16[1552,256]{1,0:T(8,128)(2,1)S(1)}, u32[]{:S(2)}, u32[]{:S(2)}) %collective-permute-start.6) | collective-permute-done | bytes 794656 | tf_op jit(solution)/shard_map/ppermute | solution.py:360
  26.4 18.2 %collective-permute-done.5.refs_2_ = bf16[1552,256]{1,0:T(8,128)(2,1)S(1)} collective-permute-done((bf16[1552,256]{1,0:T(8,128)(2,1)}, bf16[1552,256]{1,0:T(8,128)(2,1)S(1)}, u32[]{:S(2)}, u32[]{:S(2)}) %collective-permute-start.5) | collective-permute-done | bytes 794656 | tf_op jit(solution)/shard_map/ppermute | solution.py:360
  44.6 1.4 collective-permute-done.4.refs_1_
  46.0 0.0 copy-start.1
  46.0 1.1 copy-done.1
  47.1 1.9 %shard_map.72.stacked = bf16[6208,256]{1,0:T(8,128)(2,1)} custom-call(bf16[1552,256]{1,0:T(8,128)(2,1)S(1)} %copy-done.1, bf16[1552,256]{1,0:T(8,128)(2,1)S(1)} %collective-permute-done.4.refs_1_, bf16[1552,256]{1,0:T(8,128)(2,1)S(1)} %collective-permute-done.5.refs_2_, bf16[1552,256]{1,0:T(8,128)(2,1)S(1)} %collective-permute-done.6.refs_3_), custom_call_target="tpu_custom_call" | custom-call | flops 1048576 | bytes 1048576 | tf_op jit(solution)/shard_map/pallas_call | solution.py:382
  49.1 1.9 %collective-permute-start.7 = (bf16[6208,256]{1,0:T(8,128)(2,1)}, bf16[6208,256]{1,0:T(8,128)(2,1)}, u32[]{:S(2)}, u32[]{:S(2)}) collective-permute-start(bf16[6208,256]{1,0:T(8,128)(2,1)} %shard_map.72.stacked), channel_id=1, source_target_pairs={{0,1},{1,0},{2,3},{3,2},{4,5},{5,4},{6,7},{7,6},{8,9},{9,8},{10,11... | collective-permute-start | bytes 9535496 | tf_op jit(solution)/shard_map/ppermute | solution.py:388
  51.0 0.0 copy-done
  51.1 0.2 copy.15
  51.2 0.0 copy-done.2
  51.2 0.1 shard_map.68
  51.3 34.6 %all_to_all.10.got = bf16[16,72,128]{2,1,0:T(8,128)(2,1)S(1)} all-to-all(bf16[16,72,128]{2,1,0:T(8,128)(2,1)S(1)} %shard_map.68), channel_id=1, replica_groups=mesh['segment'=4,'shard'=16,'stream'=8] {'shard'}, dimensions={0} | all-to-all | bytes 589824 | tf_op jit(solution)/shard_map/all_to_all | solution.py:370
  85.9 0.1 shard_map.69
  86.0 4.4 %collective-permute-start = (bf16[8,32,256]{2,1,0:T(8,128)(2,1)S(1)}, bf16[8,32,256]{2,1,0:T(8,128)(2,1)S(1)}, u32[]{:S(2)}, u32[]{:S(2)}) collective-permute-start(bf16[8,32,256]{2,1,0:T(8,128)(2,1)S(1)} %get-tuple-element.13), channel_id=1, source_target_pairs={{0,128},{128,256},{256,384},{1,129},{129,257},{257,385},{2,130},{1... | collective-permute-start | bytes 393224 | tf_op jit(solution)/shard_map/ppermute | solution.py:360
  90.3 1.3 collective-permute-start.1
  91.6 4.5 %collective-permute-done.1.near = bf16[2,32,256]{2,1,0:T(8,128)(2,1)S(1)} collective-permute-done((bf16[2,32,256]{2,1,0:T(8,128)(2,1)S(1)}, bf16[2,32,256]{2,1,0:T(8,128)(2,1)S(1)}, u32[]{:S(2)}, u32[]{:S(2)}) %collective-permute-start.1) | collective-permute-done | bytes 32800 | tf_op jit(solution)/shard_map/ppermute | solution.py:360
  96.2 0.0 collective-permute-done.before
  96.2 2.7 %collective-permute-start.3 = (bf16[24,32,256]{2,1,0:T(8,128)(2,1)S(1)}, bf16[24,32,256]{2,1,0:T(8,128)(2,1)S(1)}, u32[]{:S(2)}, u32[]{:S(2)}) collective-permute-start(bf16[24,32,256]{2,1,0:T(8,128)(2,1)S(1)} %get-tuple-element.15.mid), channel_id=1, source_target_pairs={{8,0},{16,8},{24,16},{32,24},{40,32},{48,40},{56,48},{64,56},{72,6... | collective-permute-start | bytes 1179656 | tf_op jit(solution)/shard_map/ppermute | solution.py:402
  98.9 3.2 %collective-permute-start.2 = (bf16[24,32,256]{2,1,0:T(8,128)(2,1)S(1)}, bf16[24,32,256]{2,1,0:T(8,128)(2,1)S(1)}, u32[]{:S(2)}, u32[]{:S(2)}) collective-permute-start(bf16[24,32,256]{2,1,0:T(8,128)(2,1)S(1)} %get-tuple-element.15.mid), channel_id=1, source_target_pairs={{0,8},{8,16},{16,24},{24,32},{32,40},{40,48},{48,56},{56,64},{64,7... | collective-permute-start | bytes 1179656 | tf_op jit(solution)/shard_map/ppermute | solution.py:401
  102.1 1.3 collective-permute-start.8
  103.4 3.8 %collective-permute-done.3.right = bf16[24,32,256]{2,1,0:T(8,128)(2,1)S(1)} collective-permute-done((bf16[24,32,256]{2,1,0:T(8,128)(2,1)S(1)}, bf16[24,32,256]{2,1,0:T(8,128)(2,1)S(1)}, u32[]{:S(2)}, u32[]{:S(2)}) %collective-permute-start.3) | collective-permute-done | bytes 393248 | tf_op jit(solution)/shard_map/ppermute | solution.py:402
  107.2 1.9 %collective-permute-done.2.left = bf16[24,32,256]{2,1,0:T(8,128)(2,1)S(1)} collective-permute-done((bf16[24,32,256]{2,1,0:T(8,128)(2,1)S(1)}, bf16[24,32,256]{2,1,0:T(8,128)(2,1)S(1)}, u32[]{:S(2)}, u32[]{:S(2)}) %collective-permute-start.2) | collective-permute-done | bytes 393248 | tf_op jit(solution)/shard_map/ppermute | solution.py:401
  109.1 0.0 collective-permute-done.7.swapped
  109.1 7.0 %shard_map.73 = (bf16[20,32,256]{2,1,0:T(8,128)(2,1)S(1)}, bf16[2,32,256]{2,1,0:T(8,128)(2,1)S(1)}, bf16[4,32,256]{2,1,0:T(8,128)(2,1)S(1)}) custom-call(bf16[24,32,256]{2,1,0:T(8,128)(2,1)S(1)} %get-tuple-element.15.mid, bf16[24,32,256]{2,1,0:T(8,128)(2,1)S(1)} %collective-permute-done.2.left, bf16[24,32,256]{2,1,0:T(8,128)(2,1)S(1)} %collective-permute-done.3.right, ...), custom_call_target="tpu_custom_call" | custom-call | flops 2147483648 | bytes 4194304 | tf_op jit(solution)/shard_map/pallas_call | solution.py:280
  116.1 0.0 collective-permute-done.8.far
  116.1 1.9 %collective-permute-start.10 = (bf16[20,32,256]{2,1,0:T(8,128)(2,1)S(1)}, bf16[20,32,256]{2,1,0:T(8,128)(2,1)S(1)}, u32[]{:S(2)}, u32[]{:S(2)}) collective-permute-start(bf16[20,32,256]{2,1,0:T(8,128)(2,1)S(1)} %later.1.mid), channel_id=1, source_target_pairs={{8,0},{16,8},{24,16},{32,24},{40,32},{48,40},{56,48},{64,56},{72,6... | collective-permute-start | bytes 983048 | tf_op jit(solution)/shard_map/ppermute | solution.py:402
  118.0 3.9 %collective-permute-start.9 = (bf16[20,32,256]{2,1,0:T(8,128)(2,1)S(1)}, bf16[20,32,256]{2,1,0:T(8,128)(2,1)S(1)}, u32[]{:S(2)}, u32[]{:S(2)}) collective-permute-start(bf16[20,32,256]{2,1,0:T(8,128)(2,1)S(1)} %later.1.mid), channel_id=1, source_target_pairs={{0,8},{8,16},{16,24},{24,32},{32,40},{40,48},{48,56},{56,64},{64,7... | collective-permute-start | bytes 983048 | tf_op jit(solution)/shard_map/ppermute | solution.py:401
  122.0 0.7 collective-permute-start.11
  122.6 0.0 collective-permute-done.11.came
  122.7 1.3 collective-permute-start.12
  124.0 1.1 collective-permute-done.10.right
  125.1 1.9 %collective-permute-done.9.left = bf16[20,32,256]{2,1,0:T(8,128)(2,1)S(1)} collective-permute-done((bf16[20,32,256]{2,1,0:T(8,128)(2,1)S(1)}, bf16[20,32,256]{2,1,0:T(8,128)(2,1)S(1)}, u32[]{:S(2)}, u32[]{:S(2)}) %collective-permute-start.9) | collective-permute-done | bytes 327712 | tf_op jit(solution)/shard_map/ppermute | solution.py:401
  127.0 6.0 %shard_map.74 = (bf16[16,72,128]{2,1,0:T(8,128)(2,1)S(1)}, bf16[2,32,256]{2,1,0:T(8,128)(2,1)S(1)}) custom-call(bf16[20,32,256]{2,1,0:T(8,128)(2,1)S(1)} %later.1.mid, bf16[20,32,256]{2,1,0:T(8,128)(2,1)S(1)} %collective-permute-done.9.left, bf16[20,32,256]{2,1,0:T(8,128)(2,1)S(1)} %collective-permute-done.10.right, bf16[6208,256]{1,0:T(8,128)(2,1)} %shard_map.72.stacked, ...), custom_call_target="tpu_custom_call" | custom-call | flops 2147483648 | bytes 4194304 | tf_op jit(solution)/shard_map/pallas_call | solution.py:280
  133.0 0.0 collective-permute-done.12.wrapped
  133.0 0.1 place.1
  133.1 28.8 %all_to_all.11 = bf16[16,72,128]{2,1,0:T(8,128)(2,1)S(1)} all-to-all(bf16[16,72,128]{2,1,0:T(8,128)(2,1)S(1)} %place.1), channel_id=1, replica_groups=mesh['segment'=4,'shard'=16,'stream'=8] {'shard'}, dimensions={0} | all-to-all | bytes 589824 | tf_op jit(solution)/shard_map/all_to_all | solution.py:413
  161.9 0.8 copy.14
  162.8 0.6 reshape.16
  (10 shorter events, 0.2 us)
Async XLA Ops:
  0.6 50.4 %copy-start = (bf16[4,1,16,32,256]{4,3,2,1,0:T(8,128)(2,1)S(1)}, bf16[4,1,16,32,256]{4,3,2,1,0:T(8,128)(2,1)}, u32[]{:S(2)}) copy-start(bf16[4,1,16,32,256]{4,3,2,1,0:T(8,128)(2,1)} %param.5) | copy-start | bytes 3145732
  0.6 50.6 %copy-start.2 = (bf16[1,2,1,32,256]{4,3,2,1,0:T(8,128)(2,1)S(1)}, bf16[1,2,1,32,256]{4,3,2,1,0:T(8,128)(2,1)}, u32[]{:S(2)}) copy-start(bf16[1,2,1,32,256]{4,3,2,1,0:T(8,128)(2,1)} %param.9) | copy-start | bytes 98308
  3.6 22.8 %collective-permute-start.6 = (bf16[1552,256]{1,0:T(8,128)(2,1)}, bf16[1552,256]{1,0:T(8,128)(2,1)S(1)}, u32[]{:S(2)}, u32[]{:S(2)}) collective-permute-start(bf16[1552,256]{1,0:T(8,128)(2,1)} %shard_map.71.refs_0_), channel_id=1, source_target_pairs={{0,128},{128,256},{256,384},{384,0},{1,129},{129,257},{257,385},{3... | collective-permute-start | bytes 2383880 | tf_op jit(solution)/shard_map/ppermute | solution.py:360
  7.1 37.5 %collective-permute-start.5 = (bf16[1552,256]{1,0:T(8,128)(2,1)}, bf16[1552,256]{1,0:T(8,128)(2,1)S(1)}, u32[]{:S(2)}, u32[]{:S(2)}) collective-permute-start(bf16[1552,256]{1,0:T(8,128)(2,1)} %shard_map.71.refs_0_), channel_id=1, source_target_pairs={{0,256},{128,384},{256,0},{384,128},{1,257},{129,385},{257,1},{385... | collective-permute-start | bytes 2383880 | tf_op jit(solution)/shard_map/ppermute | solution.py:360
  11.9 34.1 %collective-permute-start.4 = (bf16[1552,256]{1,0:T(8,128)(2,1)}, bf16[1552,256]{1,0:T(8,128)(2,1)S(1)}, u32[]{:S(2)}, u32[]{:S(2)}) collective-permute-start(bf16[1552,256]{1,0:T(8,128)(2,1)} %shard_map.71.refs_0_), channel_id=1, source_target_pairs={{0,384},{128,0},{256,128},{384,256},{1,385},{129,1},{257,129},{385... | collective-permute-start | bytes 2383880 | tf_op jit(solution)/shard_map/ppermute | solution.py:360
  46.0 1.1 copy-start.1
  49.1 60.0 %collective-permute-start.7 = (bf16[6208,256]{1,0:T(8,128)(2,1)}, bf16[6208,256]{1,0:T(8,128)(2,1)}, u32[]{:S(2)}, u32[]{:S(2)}) collective-permute-start(bf16[6208,256]{1,0:T(8,128)(2,1)} %shard_map.72.stacked), channel_id=1, source_target_pairs={{0,1},{1,0},{2,3},{3,2},{4,5},{5,4},{6,7},{7,6},{8,9},{9,8},{10,11... | collective-permute-start | bytes 9535496 | tf_op jit(solution)/shard_map/ppermute | solution.py:388
  86.0 10.2 %collective-permute-start = (bf16[8,32,256]{2,1,0:T(8,128)(2,1)S(1)}, bf16[8,32,256]{2,1,0:T(8,128)(2,1)S(1)}, u32[]{:S(2)}, u32[]{:S(2)}) collective-permute-start(bf16[8,32,256]{2,1,0:T(8,128)(2,1)S(1)} %get-tuple-element.13), channel_id=1, source_target_pairs={{0,128},{128,256},{256,384},{1,129},{129,257},{257,385},{2,130},{1... | collective-permute-start | bytes 393224 | tf_op jit(solution)/shard_map/ppermute | solution.py:360
  90.3 5.8 %collective-permute-start.1 = (bf16[2,32,256]{2,1,0:T(8,128)(2,1)S(1)}, bf16[2,32,256]{2,1,0:T(8,128)(2,1)S(1)}, u32[]{:S(2)}, u32[]{:S(2)}) collective-permute-start(bf16[2,32,256]{2,1,0:T(8,128)(2,1)S(1)} %get-tuple-element.14.carry), channel_id=1, source_target_pairs={{128,0},{384,256},{129,1},{385,257},{130,2},{386,258},{131,3},{387... | collective-permute-start | bytes 98312 | tf_op jit(solution)/shard_map/ppermute | solution.py:360
  96.2 11.0 %collective-permute-start.3 = (bf16[24,32,256]{2,1,0:T(8,128)(2,1)S(1)}, bf16[24,32,256]{2,1,0:T(8,128)(2,1)S(1)}, u32[]{:S(2)}, u32[]{:S(2)}) collective-permute-start(bf16[24,32,256]{2,1,0:T(8,128)(2,1)S(1)} %get-tuple-element.15.mid), channel_id=1, source_target_pairs={{8,0},{16,8},{24,16},{32,24},{40,32},{48,40},{56,48},{64,56},{72,6... | collective-permute-start | bytes 1179656 | tf_op jit(solution)/shard_map/ppermute | solution.py:402
  98.9 10.2 %collective-permute-start.2 = (bf16[24,32,256]{2,1,0:T(8,128)(2,1)S(1)}, bf16[24,32,256]{2,1,0:T(8,128)(2,1)S(1)}, u32[]{:S(2)}, u32[]{:S(2)}) collective-permute-start(bf16[24,32,256]{2,1,0:T(8,128)(2,1)S(1)} %get-tuple-element.15.mid), channel_id=1, source_target_pairs={{0,8},{8,16},{16,24},{24,32},{32,40},{40,48},{48,56},{56,64},{64,7... | collective-permute-start | bytes 1179656 | tf_op jit(solution)/shard_map/ppermute | solution.py:401
  102.1 14.0 %collective-permute-start.8 = (bf16[4,32,256]{2,1,0:T(8,128)(2,1)S(1)}, bf16[4,32,256]{2,1,0:T(8,128)(2,1)S(1)}, u32[]{:S(2)}, u32[]{:S(2)}) collective-permute-start(bf16[4,32,256]{2,1,0:T(8,128)(2,1)S(1)} %get-tuple-element.17), channel_id=1, source_target_pairs={{256,0},{257,1},{258,2},{259,3},{260,4},{261,5},{262,6},{263,7},{2... | collective-permute-start | bytes 196616 | tf_op jit(solution)/shard_map/ppermute | solution.py:360
  116.1 9.0 %collective-permute-start.10 = (bf16[20,32,256]{2,1,0:T(8,128)(2,1)S(1)}, bf16[20,32,256]{2,1,0:T(8,128)(2,1)S(1)}, u32[]{:S(2)}, u32[]{:S(2)}) collective-permute-start(bf16[20,32,256]{2,1,0:T(8,128)(2,1)S(1)} %later.1.mid), channel_id=1, source_target_pairs={{8,0},{16,8},{24,16},{32,24},{40,32},{48,40},{56,48},{64,56},{72,6... | collective-permute-start | bytes 983048 | tf_op jit(solution)/shard_map/ppermute | solution.py:402
  118.0 9.0 %collective-permute-start.9 = (bf16[20,32,256]{2,1,0:T(8,128)(2,1)S(1)}, bf16[20,32,256]{2,1,0:T(8,128)(2,1)S(1)}, u32[]{:S(2)}, u32[]{:S(2)}) collective-permute-start(bf16[20,32,256]{2,1,0:T(8,128)(2,1)S(1)} %later.1.mid), channel_id=1, source_target_pairs={{0,8},{8,16},{16,24},{24,32},{32,40},{40,48},{48,56},{56,64},{64,7... | collective-permute-start | bytes 983048 | tf_op jit(solution)/shard_map/ppermute | solution.py:401
  122.0 0.7 collective-permute-start.11
  122.7 10.3 %collective-permute-start.12 = (bf16[2,32,256]{2,1,0:T(8,128)(2,1)S(1)}, bf16[2,32,256]{2,1,0:T(8,128)(2,1)S(1)}, u32[]{:S(2)}, u32[]{:S(2)}) collective-permute-start(bf16[2,32,256]{2,1,0:T(8,128)(2,1)S(1)} %shard_map.75), channel_id=1, source_target_pairs={{384,0},{256,128},{385,1},{257,129},{386,2},{258,130},{387,3},{259... | collective-permute-start | bytes 98312 | tf_op jit(solution)/shard_map/ppermute | solution.py:360
